TPU v7x, 32 devices: a whole 2x2x4 slice. The times are simulated.
32 devices in a mesh: cam: 16 (over z, y, core), frame: 2 (over x).
Axes of the slice: x: 2, y: 2, z: 4, core: 2. Of those that a mesh axis runs over, the one named last changes fastest.
Arguments:
- frames: bfloat16 [16, 64, 3, 4096], P('cam', 'frame'), may hold values from -6 to 6
- conv1_w: bfloat16 [27, 128], replicated, may hold values from -1.25 to 1.25
- conv2_w: bfloat16 [1152, 256], replicated, may hold values from -0.1875 to 0.1875
- tile_w: bfloat16 [256, 128], replicated, may hold values from -0.375 to 0.375
- vis_subject: int32 [16, 64, 12], P('cam', 'frame'), may hold values from 0 to 63, as said below
- part_count: int32 [16, 64, 12], P('cam', 'frame'), may hold values from 6 to 8
- part_region: int32 [16, 64, 12, 8], P('cam', 'frame'), may hold values from 0 to 15
- subject_slot: int32 [64], replicated, may hold values from 0 to 63, as said below
- qkv_w: bfloat16 [1024, 3072], replicated, may hold values from -0.1875 to 0.1875
- out_w: bfloat16 [1024, 1024], replicated, may hold values from -0.1875 to 0.1875
- key_bias: float32 [64, 16, 64], P('cam'), may hold values from -2 to 237
Outputs:
- posed: bfloat16 [64, 64, 1024], P('cam', 'frame')
Inputs may be any that keep to these rules, and one draw needn't show every extreme that they name: `vis_subject`: each camera frame lists 12 distinct subjects. Rows of the subject-owned arrays form blocks of 4 (the rows of one index of cam); one list names at most 2 subjects whose rows lie in one block, and for each aligned block of 32 frames one row block, drawn for it, has exactly 2 subjects in every camera's list of every frame of it. `subject_slot`: A permutation of the subjects' numbers.
All inputs are finite; a program needn't handle non-finite values.
Results may differ from a plain program's by a relative error of at most 0.0085.
Values may be sent and summed in bfloat16 or wider, within the bound.
No kernel may reach another device: no remote copies, remote signals or barrier semaphores. Data moves between devices by JAX's collectives and lax.ppermute only.
A program may use at most 64 MiB of HBM per device.

v0:
```python
import math

import jax
import jax.numpy as jnp
from jax import lax
from jax.sharding import PartitionSpec as P

IMG = 64
RGRID = 4
C1 = 128
C2 = 256
TILE = 128
HEADS = 16
SUBJ_DEV = 4
PER_OWN = 2


EPS = 1e-05
NEG_START = -1e30


def conv_features(pictures, conv1_w, conv2_w):
    amount = pictures.shape[0]
    images = pictures.reshape(amount, 3, IMG, IMG)
    section_one = lax.conv_general_dilated(
        images,
        conv1_w.reshape(3, 3, 3, C1),
        (2, 2),
        ((1, 1), (1, 1)),
        dimension_numbers=("NCHW", "HWIO", "NHWC"),
        preferred_element_type=jnp.float32,
    )
    section_one = jax.nn.relu(section_one).astype(jnp.bfloat16)
    section_two = lax.conv_general_dilated(
        section_one,
        conv2_w.reshape(3, 3, C1, C2),
        (2, 2),
        ((1, 1), (1, 1)),
        dimension_numbers=("NHWC", "HWIO", "NHWC"),
        preferred_element_type=jnp.float32,
    )
    section_two = jax.nn.relu(section_two)
    patch_side = IMG // (4 * RGRID)
    pooled = jnp.mean(
        section_two.reshape(amount, RGRID, patch_side, RGRID, patch_side, C2), axis=(2, 4)
    )
    return pooled.reshape(amount, RGRID * RGRID, C2).astype(jnp.bfloat16)


def select_parts(features, part_region, part_count):
    frames_here, listed, part_total = part_region.shape
    regions = features.shape[1]
    visible = jnp.arange(part_total, dtype=jnp.int32)[None, None, :] < part_count[:, :, None]
    chooser = (part_region[:, :, :, None] == jnp.arange(regions, dtype=jnp.int32)) & visible[
        :, :, :, None
    ]
    chooser = chooser.astype(jnp.bfloat16).reshape(frames_here, listed * part_total, regions)
    picked = jnp.einsum("fer,frc->fec", chooser, features, preferred_element_type=jnp.float32)
    return picked.astype(jnp.bfloat16).reshape(frames_here * listed, part_total * features.shape[2])


def build_buffers(payload, vis_subject, subject_slot, owners, frames_here):
    listed = vis_subject.shape[1]
    entries = frames_here * listed
    subjects = subject_slot.shape[0]
    flat_ids = vis_subject.reshape(entries)
    slot_rows = jnp.sum(
        jnp.where(
            flat_ids[:, None] == jnp.arange(subjects, dtype=jnp.int32), subject_slot[None, :], 0
        ),
        axis=1,
    )
    owner_index = slot_rows // SUBJ_DEV
    member = (owner_index[:, None] == jnp.arange(owners, dtype=jnp.int32)).astype(jnp.int32)
    arrival = jnp.sum((jnp.cumsum(member, axis=0) - 1) * member, axis=1)
    capacity = PER_OWN * frames_here
    target = owner_index * capacity + arrival
    source = (
        jnp.full((owners * capacity,), entries, jnp.int32)
        .at[target]
        .set(jnp.arange(entries, dtype=jnp.int32))
    )
    padded = jnp.concatenate([payload, jnp.zeros((1, payload.shape[1]), payload.dtype)], axis=0)
    frame_of = jnp.arange(entries, dtype=jnp.int32) // listed
    placement_code = slot_rows % SUBJ_DEV * frames_here + frame_of
    codes = jnp.concatenate([placement_code, jnp.full((1,), SUBJ_DEV * frames_here, jnp.int32)])
    outgoing = padded[source].reshape(owners, capacity, payload.shape[1])
    return (outgoing, codes[source].reshape(owners, capacity))


def collect_tokens(received, arrived, rows):
    flat_rows = received.reshape(-1, received.shape[2])
    picker = (jnp.arange(rows, dtype=jnp.int32)[:, None] == arrived.reshape(1, -1)).astype(
        jnp.bfloat16
    )
    return jnp.dot(picker, flat_rows, preferred_element_type=jnp.float32)


def per_device(
    frames,
    conv1_w,
    conv2_w,
    tile_w,
    vis_subject,
    part_count,
    part_region,
    subject_slot,
    qkv_w,
    out_w,
    key_bias,
):
    pictures = frames[0]
    frames_here = pictures.shape[0]
    owners = lax.axis_size("cam")
    pooled = conv_features(pictures, conv1_w, conv2_w)
    projected = jnp.dot(pooled.reshape(-1, C2), tile_w, preferred_element_type=jnp.float32)
    tiles = projected.astype(jnp.bfloat16).reshape(frames_here, -1, TILE)
    payload = select_parts(tiles, part_region[0], part_count[0])
    outgoing, codes = build_buffers(payload, vis_subject[0], subject_slot, owners, frames_here)
    received, arrived = (
        lax.all_to_all(outgoing, "cam", split_axis=0, concat_axis=0, tiled=True),
        lax.all_to_all(codes, "cam", split_axis=0, concat_axis=0, tiled=True),
    )
    tokens = collect_tokens(received, arrived, SUBJ_DEV * frames_here)
    width = tokens.shape[1]
    head_size = width // HEADS
    score_scale = 1.0 / math.sqrt(head_size)
    normed = (tokens * lax.rsqrt(jnp.mean(tokens * tokens, axis=1, keepdims=True) + EPS)).astype(
        jnp.bfloat16
    )
    mixed = jnp.dot(normed, qkv_w, preferred_element_type=jnp.float32).astype(jnp.bfloat16)
    queries = mixed[:, :width].reshape(SUBJ_DEV, frames_here, HEADS, head_size)
    key_rows = mixed[:, width : 2 * width].reshape(SUBJ_DEV, frames_here, width)
    value_rows = mixed[:, 2 * width :].reshape(SUBJ_DEV, frames_here, width)
    row_top = jnp.full((SUBJ_DEV, HEADS, frames_here), NEG_START, jnp.float32)
    key_piece = lax.all_gather(key_rows, "frame", axis=1, tiled=True)
    value_piece = lax.all_gather(value_rows, "frame", axis=1, tiled=True)
    span = key_piece.shape[1]
    scores = (
        jnp.einsum(
            "sqhd,skhd->shqk",
            queries,
            key_piece.reshape(SUBJ_DEV, span, HEADS, head_size),
            preferred_element_type=jnp.float32,
        )
        * score_scale
    )
    scores = scores + key_bias[:, :, None, :]
    new_top = jnp.maximum(row_top, jnp.max(scores, axis=3))
    weights = jnp.exp(scores - new_top[..., None])
    denominator = jnp.sum(weights, axis=3)
    numerator = jnp.einsum(
        "shqk,skhd->shqd",
        weights.astype(jnp.bfloat16),
        value_piece.reshape(SUBJ_DEV, span, HEADS, head_size),
        preferred_element_type=jnp.float32,
    )
    row_top, denominator, numerator = (new_top, denominator, numerator)
    attended = numerator / denominator[..., None]
    attended = (
        jnp.transpose(attended, (0, 2, 1, 3))
        .reshape(SUBJ_DEV * frames_here, width)
        .astype(jnp.bfloat16)
    )
    posed = tokens + jnp.dot(attended, out_w, preferred_element_type=jnp.float32)
    return posed.astype(jnp.bfloat16).reshape(SUBJ_DEV, frames_here, width)


def solution(mesh):
    in_specs = (
        P("cam", "frame", None, None),
        P(),
        P(),
        P(),
        P("cam", "frame", None),
        P("cam", "frame", None),
        P("cam", "frame", None, None),
        P(),
        P(),
        P(),
        P("cam", None, None),
    )
    out_specs = P("cam", "frame", None)
    return jax.shard_map(
        per_device, mesh=mesh, in_specs=in_specs, out_specs=out_specs, check_vma=False
    )
```

profile of v0, /device:TPU:12, one launch (start us, length us, event | category | flops | bytes accessed | tf_op | source)
XLA Modules:
  0.0 141.6 jit_solution(5429485537469918314)
XLA Ops:
  0.0 0.9 copy.44
  0.9 0.1 eq.70
  1.0 0.8 select_reduce_fusion
  1.8 0.9 reduce-window.6
  2.7 0.2 slice_reduce_fusion
  3.0 0.1 fusion.21
  3.1 2.9 %scatter_custom_fusion = s32[1024]{0:T(1024)S(1)} fusion(s32[384]{0:T(512)S(1)} %fusion.35, s32[384]{0:T(512)S(1)} %iota.33, s32[]{:T(128)} %constant.64.clone.1), kind=kCustom, calls=%fused_computation.78 | custom fusion | bytes 4100 | tf_op jit(solution)/shard_map/scatter | solution.py:81
  6.1 0.0 copy-start.5
  6.1 0.0 copy-start.7
  6.1 6.9 %gather_fusion = s32[1024]{0:T(1024)S(1)} fusion(s32[385]{0:T(512)S(1)} %pad_add_fusion, s32[1024]{0:T(1024)S(1)} %fusion.23), kind=kCustom, calls=%fused_computation | custom fusion | bytes 12288 | tf_op jit(solution)/shard_map/gather | solution.py:88
  13.0 0.7 all_to_all.9
  13.6 6.2 %all-to-all-start = ((s32[16,1,64]{2,1,0:T(1,128)}), s32[16,1,64]{2,1,0:T(1,128)S(1)}, u32[]{:S(2)}, u32[]{:S(2)}) async-start(s32[16,1,64]{2,1,0:T(1,128)} %all_to_all.9), calls=%async_computation | async-start | bytes 16384 | tf_op jit(solution)/shard_map/all_to_all | solution.py:122
  19.9 4.7 %copy.54 = bf16[1,32,3,4096]{1,2,3,0:T(4,128)(2,1)} copy(bf16[1,32,3,4096]{3,1,2,0:T(8,128)(2,1)S(1)} %copy-done.1) | data formatting | bytes 1572864 | tf_op jit(solution)/shard_map/reshape;squeeze | solution.py:24
  24.6 15.4 %broadcast_maximum_fusion = f32[32,16,16,256]{3,0,2,1:T(8,128)} fusion(bf16[3,3,128,256]{3,2,1,0:T(8,128)(2,1)S(1)} %bitcast.76, bf16[32,3,64,64]{0,1,3,2:T(4,128)(2,1)} %bitcast.68, bf16[3,3,3,128]{3,2,1,0:T(4,128)(2,1)S(1)} %reshape.171), kind=kOutput, calls=%fused_computation.6 | convolution fusion | flops 4864892928 | bytes 9771776 | tf_op jit(solution)/shard_map/conv_general_dilated | solution.py:34
  40.0 4.4 %reduce_sum.56 = f32[32,4,4,256]{3,0,2,1:T(8,128)S(1)} reduce(f32[32,4,4,4,4,256]{5,0,4,3,2,1:T(8,128)} %bitcast.67, f32[]{:T(128)} %constant.69.clone.1), dimensions={2,4}, to_apply=%region_5.6 | reduce | flops 1966080 | bytes 8912900 | tf_op jit(solution)/shard_map/reduce_sum | solution.py:44
  44.5 0.2 copy.49
  44.7 0.1 convert_element_type.44
  44.8 0.1 copy.46
  44.9 0.1 lt.50
  45.0 0.1 bitcast_compare_fusion
  45.1 0.1 copy.47
  45.1 0.0 copy-done.2
  45.1 0.2 convolution_convert_fusion.2
  45.4 0.6 convolution_convert_fusion.1
  46.0 1.2 reshape.175
  47.2 1.2 concatenate.7
  48.4 5.4 %gather_fusion.1 = bf16[1024,1024]{1,0:T(8,128)(2,1)} fusion(bf16[385,1024]{1,0:T(8,128)(2,1)S(1)} %concatenate.7, s32[1024]{0:T(1024)S(1)} %fusion.23), kind=kCustom, calls=%fused_computation.1 | custom fusion | bytes 4198400 | tf_op jit(solution)/shard_map/gather | solution.py:87
  53.8 0.0 all-to-all-done
  53.8 6.0 %all-to-all-start.1 = ((bf16[16,64,1024]{2,1,0:T(8,128)(2,1)}), bf16[16,64,1024]{2,1,0:T(8,128)(2,1)}, u32[]{:S(2)}, u32[]{:S(2)}) async-start(bf16[16,64,1024]{2,1,0:T(8,128)(2,1)} %bitcast.66), calls=%async_computation.1 | async-start | bytes 4194304 | tf_op jit(solution)/shard_map/all_to_all | solution.py:121
  59.8 0.5 broadcast.219
  60.3 0.7 reduce.7
  61.0 0.1 eq.80
  61.1 46.0 %all-to-all-done.1 = bf16[16,64,1024]{2,1,0:T(8,128)(2,1)} async-done(((bf16[16,64,1024]{2,1,0:T(8,128)(2,1)}), bf16[16,64,1024]{2,1,0:T(8,128)(2,1)}, u32[]{:S(2)}, u32[]{:S(2)}) %all-to-all-start.1) | async-done | bytes 2097184 | tf_op jit(solution)/shard_map/all_to_all | solution.py:121
  107.0 2.1 %multiply_reduce_fusion = (f32[128]{0:T(128)S(1)}, f32[128,1024]{1,0:T(8,128)S(1)}) fusion(bf16[1024,1024]{1,0:T(8,128)(2,1)} %bitcast.9, s32[1024]{0:T(1024)S(1)} %eq.80), kind=kOutput, calls=%fused_computation.25 | convolution fusion | flops 268828544 | bytes 2626048 | tf_op jit(solution)/shard_map/dot_general | solution.py:96
  109.2 3.8 %convolution_convert_fusion = bf16[128,3072]{1,0:T(8,128)(2,1)S(1)} fusion(bf16[1024,3072]{1,0:T(8,128)(2,1)} %param.19, f32[128,1024]{1,0:T(8,128)S(1)} %get-tuple-element.11, f32[128]{0:T(128)S(1)} %add_rsqrt_fusion), kind=kOutput, calls=%fused_computation.7 | convolution fusion | flops 805961728 | bytes 7602688 | tf_op jit(solution)/shard_map/dot_general | solution.py:131
  113.0 0.0 copy-start.4
  113.0 0.8 fusion.37
  113.8 9.3 %all_gather.7 = bf16[4,64,1024]{2,1,0:T(8,128)(2,1)S(1)} all-gather(bf16[4,32,1024]{2,1,0:T(8,128)(2,1)S(1)} %bitcast.70), channel_id=1, replica_groups=mesh['cam'=16,'frame'=2] {'frame'}, dimensions={1}, use_global_device_ids=true | all-gather | bytes 786432 | tf_op jit(solution)/shard_map/all_gather | solution.py:137
  123.0 1.7 %reshape.182 = bf16[4,64,16,64]{3,2,1,0:T(8,128)(2,1)} reshape(bf16[4,64,1024]{2,1,0:T(8,128)(2,1)S(1)} %all_gather.7) | data formatting | bytes 1048576 | tf_op jit(solution)/shard_map/reshape | solution.py:155
  124.7 8.6 %all_gather.6 = bf16[4,64,1024]{2,1,0:T(8,128)(2,1)S(1)} all-gather(bf16[4,32,1024]{2,1,0:T(8,128)(2,1)} %bitcast.69), channel_id=1, replica_groups=mesh['cam'=16,'frame'=2] {'frame'}, dimensions={1}, use_global_device_ids=true | all-gather | bytes 786432 | tf_op jit(solution)/shard_map/all_gather | solution.py:136
  133.3 1.7 %reshape.180 = bf16[4,64,16,64]{3,2,1,0:T(8,128)(2,1)} reshape(bf16[4,64,1024]{2,1,0:T(8,128)(2,1)S(1)} %all_gather.6) | data formatting | bytes 1048576 | tf_op jit(solution)/shard_map/reshape | solution.py:143
  135.0 0.3 reshape.178
  135.3 2.0 %fusion.38 = (f32[4,16,32]{2,1,0:T(8,128)S(1)}, f32[4,16,32,64]{3,2,1,0:T(8,128)S(1)}) fusion(f32[4,16,64]{2,1,0:T(8,128)S(1)} %copy-done.4, bf16[4,64,16,64]{3,2,1,0:T(8,128)(2,1)} %reshape.180, bf16[4,32,16,64]{3,2,1,0:T(8,128)(2,1)S(1)} %reshape.178), kind=kOutput, calls=%fused_computation.88 | convolution fusion | flops 17168384 | bytes 1335296 | tf_op jit(solution)/shard_map/sqhd,skhd->shqk/dot_general | solution.py:140
  137.3 0.6 fusion.8
  138.0 1.9 %fusion.4 = bf16[4,32,16,64]{3,1,2,0:T(8,128)(2,1)S(1)} fusion(bf16[4,64,16,64]{3,2,1,0:T(8,128)(2,1)} %reshape.182, f32[4,16,32,64]{3,2,1,0:T(8,128)S(1)} %get-tuple-element.13, f32[4,32,16]{1,2,0:T(8,128)S(1)} %bitcast.73, f32[4,16,32]{2,1,0:T(8,128)S(1)} %broadcast_maximum_fusion.1), kind=kOutput, calls=%fused_computation.13 | convolution fusion | flops 17301504 | bytes 1327104 | tf_op jit(solution)/shard_map/shqk,skhd->shqd/dot_general | solution.py:152
  139.8 0.2 copy.53
  140.0 0.3 convert_element_type.51
  140.4 1.2 fusion.5
  (26 shorter events, 0.2 us)
Async XLA Ops:
  0.0 140.4 %copy-start = (bf16[1024,1024]{1,0:T(8,128)(2,1)S(1)}, bf16[1024,1024]{1,0:T(8,128)(2,1)}, u32[]{:S(2)}) copy-start(bf16[1024,1024]{1,0:T(8,128)(2,1)} %param.20) | copy-start | bytes 6291460
  0.0 19.9 %copy-start.1 = (bf16[1,32,3,4096]{3,1,2,0:T(8,128)(2,1)S(1)}, bf16[1,32,3,4096]{3,1,2,0:T(8,128)(2,1)}, u32[]{:S(2)}) copy-start(bf16[1,32,3,4096]{3,1,2,0:T(8,128)(2,1)} %param.11) | copy-start | bytes 2359300
  6.1 18.6 %copy-start.5 = (bf16[27,128]{1,0:T(8,128)(2,1)S(1)}, bf16[27,128]{1,0:T(8,128)(2,1)}, u32[]{:S(2)}) copy-start(bf16[27,128]{1,0:T(8,128)(2,1)} %param.12) | copy-start | bytes 20740
  6.1 18.6 %copy-start.7 = (bf16[1152,256]{1,0:T(8,128)(2,1)S(1)}, bf16[1152,256]{1,0:T(8,128)(2,1)}, u32[]{:S(2)}) copy-start(bf16[1152,256]{1,0:T(8,128)(2,1)} %param.13) | copy-start | bytes 1769476
  13.6 40.1 %all-to-all-start = ((s32[16,1,64]{2,1,0:T(1,128)}), s32[16,1,64]{2,1,0:T(1,128)S(1)}, u32[]{:S(2)}, u32[]{:S(2)}) async-start(s32[16,1,64]{2,1,0:T(1,128)} %all_to_all.9), calls=%async_computation | async-start | bytes 16384 | tf_op jit(solution)/shard_map/all_to_all | solution.py:122
  40.0 4.8 %copy-start.3 = (s32[1,32,12,8]{1,3,2,0:T(8,128)S(1)}, s32[1,32,12,8]{1,3,2,0:T(8,128)}, u32[]{:S(2)}) copy-start(s32[1,32,12,8]{1,3,2,0:T(8,128)} %param.17) | copy-start | bytes 36868
  40.0 4.8 %copy-start.6 = (s32[1,32,12]{1,0,2:T(1,128)S(1)}, s32[1,32,12]{1,0,2:T(1,128)}, u32[]{:S(2)}) copy-start(s32[1,32,12]{1,0,2:T(1,128)} %param.16) | copy-start | bytes 4612
  40.0 5.1 %copy-start.2 = (bf16[256,128]{1,0:T(8,128)(2,1)S(1)}, bf16[256,128]{1,0:T(8,128)(2,1)}, u32[]{:S(2)}) copy-start(bf16[256,128]{1,0:T(8,128)(2,1)} %param.14) | copy-start | bytes 196612
  53.8 53.3 %all-to-all-start.1 = ((bf16[16,64,1024]{2,1,0:T(8,128)(2,1)}), bf16[16,64,1024]{2,1,0:T(8,128)(2,1)}, u32[]{:S(2)}, u32[]{:S(2)}) async-start(bf16[16,64,1024]{2,1,0:T(8,128)(2,1)} %bitcast.66), calls=%async_computation.1 | async-start | bytes 4194304 | tf_op jit(solution)/shard_map/all_to_all | solution.py:121
  113.0 22.3 %copy-start.4 = (f32[4,16,64]{2,1,0:T(8,128)S(1)}, f32[4,16,64]{2,1,0:T(8,128)}, u32[]{:S(2)}) copy-start(f32[4,16,64]{2,1,0:T(8,128)} %param.21) | copy-start | bytes 49156
where the time goes:
time: 142 us
  waiting for transfers between devices  46 us (32%)
  local copies, waits for them, and re-layouts  30.4 us (21%)
  matrix products  27.1 us (19%)
  blocking collectives  17.9 us (13%)
  starting transfers between devices  12.3 us (9%)
  other arithmetic  7.7 us (5%)
    all_to_all x1, waiting for transfers between devices, per_device(): lax.all_to_all(outgoing, 'cam', split_axis=0, concat_axis=0, tiled=True)  46 us
    conv_general_dilated x1, matrix products, conv_features(): lax.conv_general_dilated(section_one, conv2_w.reshape(3, 3, C1, C2), (2,...  15.4 us
    all_gather x1, blocking collectives, per_device(): value_piece = lax.all_gather(value_rows, 'frame', axis=1, tiled=True)  9.25 us
    all_gather x1, blocking collectives, per_device(): key_piece = lax.all_gather(key_rows, 'frame', axis=1, tiled=True)  8.6 us
    gather x1, local copies, waits for them, and re-layouts, build_buffers(): return (outgoing, codes[source].reshape(owners, capacity))  6.87 us
    all_to_all x1, starting transfers between devices, per_device(): lax.all_to_all(codes, 'cam', split_axis=0, concat_axis=0, tiled=True)  6.24 us
    all_to_all x1, starting transfers between devices, per_device(): lax.all_to_all(outgoing, 'cam', split_axis=0, concat_axis=0, tiled=True)  6.01 us
    gather x1, local copies, waits for them, and re-layouts, build_buffers(): outgoing = padded[source].reshape(owners, capacity, payload.shape[1])  5.39 us
  transfers between devices with their start and end apart: 2, of which 1 were waited for; matrix products, arithmetic and copies ran while one was open for 25% of the time, Pallas kernels for 0%

commit v1 on v0

v1 whole, which is shorter than its diff:
```python
import functools
import math

import jax
import jax.numpy as jnp
import numpy as np
from jax import lax
from jax.experimental import pallas as pl
from jax.experimental.pallas import tpu as pltpu
from jax.sharding import PartitionSpec as P

IMG = 64
RGRID = 4
HEADS = 16
SUBJ_DEV = 4
EPS = 1e-05

LANES = 128
BF = jnp.bfloat16
F32 = jnp.float32
OUT1 = IMG // 2
OUT2 = IMG // 4
PATCH = OUT2 // RGRID
REGIONS = RGRID * RGRID
GROUP = 8
GROUPS = OUT1 // GROUP
SEG = 21
VMEM_ALL = pl.BlockSpec(memory_space=pltpu.VMEM)


def pack_table():
    table = np.zeros((3 * LANES, GROUPS * LANES), np.float32)
    for group in range(GROUPS):
        for row in range(2):
            for ch in range(3):
                for pos in range(2 * GROUP + 1):
                    pixel = 2 * GROUP * group - 1 + pos
                    if 0 <= pixel < IMG:
                        source = ch * LANES + row * IMG + pixel
                        table[source, group * LANES + row * IMG + ch * SEG + pos] = 1.0
    return table


def tap_table():
    table = np.zeros((GROUP, 2 * LANES, 32), np.float32)
    for column in range(GROUP):
        for dy in range(3):
            base = {1: 0, 2: IMG, 0: LANES + IMG}[dy]
            for dx in range(3):
                for ch in range(3):
                    lane = base + ch * SEG + 2 * column + dx
                    table[column, lane, dy * 9 + dx * 3 + ch] = 1.0
    return table.reshape(GROUP * 2 * LANES, 32)


def camera_kernel(
    x_ref, pack_ref, tap_ref, w1_ref, w2_ref, wt_ref, vis_ref, count_ref, region_ref, slot_ref,
    out_ref, packed, wide, cells, part, *, subjects, parts
):
    frames_here = x_ref.shape[1]
    rows = OUT1 * frames_here
    listed = vis_ref.shape[1]
    lanes = listed * parts
    expand = (
        lax.broadcasted_iota(jnp.int32, (listed, lanes), 1) // parts
        == lax.broadcasted_iota(jnp.int32, (listed, lanes), 0)
    ).astype(BF)

    def spread(ref):
        return jnp.dot(ref[...].astype(F32).astype(BF), expand, preferred_element_type=F32)

    who = spread(vis_ref).astype(jnp.int32)
    count = spread(count_ref).astype(jnp.int32)
    part_of = lax.broadcasted_iota(jnp.int32, (frames_here, lanes), 1) % parts
    code = jnp.where(part_of < count, region_ref[...] + 1, 0)
    row_of = jnp.zeros((frames_here, lanes), jnp.int32)
    for subject in range(subjects):
        row_of = jnp.where(who == subject, slot_ref[subject], row_of)
    blocks = -(-lanes // LANES)
    fill = blocks * LANES - lanes
    if fill:
        zeros = jnp.zeros((frames_here, fill), jnp.int32)
        code = jnp.concatenate([code, zeros], axis=1)
        row_of = jnp.concatenate([row_of, zeros], axis=1)
    base = REGIONS * frames_here
    for k, array in enumerate((code, row_of)):
        for block in range(blocks):
            at = base + (k * blocks + block) * frames_here
            out_ref[at : at + frames_here, :] = (
                array[:, block * LANES : (block + 1) * LANES].astype(F32).astype(BF)
            )

    for column in range(GROUP):
        wide[:, column * LANES : (column + 1) * LANES] = jnp.dot(
            tap_ref[column * 2 * LANES : (column + 1) * 2 * LANES, :],
            w1_ref[...],
            preferred_element_type=F32,
        ).astype(BF)
    packed[:, 0:frames_here, :] = jnp.zeros((GROUPS, frames_here, LANES), BF)
    images = jnp.concatenate(
        [
            jnp.concatenate(
                [x_ref[ch, :, y * LANES : (y + 1) * LANES] for ch in range(3)], axis=1
            )
            for y in range(OUT1)
        ],
        axis=0,
    )
    for group in range(GROUPS):
        packed[group, frames_here:, :] = jnp.dot(
            images, pack_ref[:, group * LANES : (group + 1) * LANES], preferred_element_type=F32
        ).astype(BF)
    cells[0] = jnp.zeros(cells.shape[1:], BF)
    cells[:, 1, 0] = jnp.zeros((cells.shape[0],) + cells.shape[3:], BF)
    for group in range(GROUPS):
        lhs = jnp.concatenate(
            [packed[group, frames_here:, :], packed[group, 0:rows, :]], axis=1
        )
        for pair in range(GROUP // 2):
            both = jnp.dot(
                lhs, wide[:, pair * 2 * LANES : (pair + 1) * 2 * LANES], preferred_element_type=F32
            )
            both = jnp.maximum(both, 0.0).astype(BF)
            at = group * (GROUP // 2) + pair
            cells[1:, 0, at] = both[:, :LANES].reshape(OUT1, frames_here, LANES)
            cells[1:, 1, at + 1] = both[:, LANES:].reshape(OUT1, frames_here, LANES)

    width = w2_ref.shape[1]
    for ry in range(RGRID):
        total = jnp.zeros((RGRID, frames_here, width), F32)
        for y in range(ry * PATCH, (ry + 1) * PATCH):
            taps = []
            for dy in range(3):
                for parity, start in ((1, 0), (0, 0), (1, 1)):
                    taps.append(
                        cells[2 * y + dy, parity, start : start + OUT2].reshape(
                            OUT2 * frames_here, LANES
                        )
                    )
            two = jnp.dot(
                jnp.concatenate(taps, axis=1), w2_ref[...], preferred_element_type=F32
            )
            two = jnp.maximum(two, 0.0).reshape(RGRID, PATCH, frames_here, width)
            for k in range(PATCH):
                total = total + two[:, k]
        pooled = (total * (1.0 / (PATCH * PATCH))).astype(BF)
        tiles = jnp.dot(
            pooled.reshape(RGRID * frames_here, width), wt_ref[...], preferred_element_type=F32
        )
        for rx in range(RGRID):
            part[pl.ds(ry * RGRID + rx, frames_here, stride=REGIONS), :] = tiles[
                rx * frames_here : (rx + 1) * frames_here
            ]
    out_ref[0:base, :] = part[...].astype(BF)


def camera_tiles(frames, conv1_w, conv2_w, tile_w, vis_subject, part_count, part_region, slots):
    frames_here = frames.shape[1]
    listed, parts = part_region.shape[2:]
    blocks = -(-listed * parts // LANES)
    images = jnp.transpose(frames[0], (1, 0, 2))
    taps = jnp.pad(conv1_w, ((0, 32 - conv1_w.shape[0]), (0, 0)))
    return pl.pallas_call(
        functools.partial(camera_kernel, subjects=slots.shape[0], parts=parts),
        out_shape=jax.ShapeDtypeStruct(((REGIONS + 2 * blocks) * frames_here, LANES), BF),
        in_specs=[VMEM_ALL] * 9 + [pl.BlockSpec(memory_space=pltpu.SMEM)],
        out_specs=VMEM_ALL,
        scratch_shapes=[
            pltpu.VMEM((GROUPS, (OUT1 + 1) * frames_here, LANES), BF),
            pltpu.VMEM((2 * LANES, GROUP * LANES), BF),
            pltpu.VMEM((OUT1 + 1, 2, OUT2 + 1, frames_here, LANES), BF),
            pltpu.VMEM((REGIONS * frames_here, LANES), F32),
        ],
        compiler_params=pltpu.CompilerParams(vmem_limit_bytes=50 << 20),
    )(
        images,
        jnp.asarray(pack_table(), BF),
        jnp.asarray(tap_table(), BF),
        taps,
        conv2_w,
        tile_w,
        vis_subject[0],
        part_count[0],
        part_region[0].reshape(frames_here, listed * parts),
        slots,
    )


def exchange(payload):
    cams = lax.axis_size("cam")
    if cams & (cams - 1):
        gathered = lax.all_gather(payload, "cam", axis=0, tiled=False)
        return [gathered[c] for c in range(cams)]

    def swap(array, bits):
        return lax.ppermute(array, "cam", [(i, i ^ bits) for i in range(cams)])

    pieces = [payload] + [swap(payload, bits) for bits in range(2, cams, 2)]
    return pieces + [swap(piece, 1) for piece in pieces]


def token_kernel(me_ref, *refs, cams, parts, frames_here):
    pieces = refs[:cams]
    tokens_ref, normed_ref, marks, spots, picks, summed = refs[cams:]
    blocks = (pieces[0].shape[0] // frames_here - REGIONS) // 2
    lanes = blocks * LANES
    places = SUBJ_DEV * parts
    first = me_ref[0] * SUBJ_DEV
    base = REGIONS * frames_here
    from_lane = lax.broadcasted_iota(jnp.int32, (SUBJ_DEV * lanes, LANES), 0)
    to_lane = lax.broadcasted_iota(jnp.int32, (SUBJ_DEV * lanes, LANES), 1)
    fold = (
        (from_lane % parts == to_lane % parts) & (from_lane // lanes == to_lane // parts)
    ).astype(BF)
    codes = []
    for piece in pieces:

        def field(k):
            return jnp.concatenate(
                [
                    piece[
                        base + (k * blocks + b) * frames_here : base
                        + (k * blocks + b + 1) * frames_here,
                        :,
                    ].astype(F32)
                    for b in range(blocks)
                ],
                axis=1,
            )

        code, row = field(0), field(1)
        codes.append(
            jnp.concatenate(
                [
                    jnp.where(row == (first + s).astype(F32), code, 0.0).astype(BF)
                    for s in range(SUBJ_DEV)
                ],
                axis=1,
            )
        )
    marks[...] = jnp.dot(jnp.concatenate(codes, axis=0), fold, preferred_element_type=F32)
    for f in range(frames_here):
        found = marks[pl.ds(f, cams, stride=frames_here), :]
        spots[f * places : (f + 1) * places, :] = found.T[:places].astype(BF)
    widen = (
        lax.broadcasted_iota(jnp.int32, (cams, cams * REGIONS), 1) // REGIONS
        == lax.broadcasted_iota(jnp.int32, (cams, cams * REGIONS), 0)
    ).astype(BF)
    spread = jnp.dot(spots[...], widen, preferred_element_type=F32)
    region = lax.broadcasted_iota(jnp.int32, spread.shape, 1) % REGIONS + 1
    picks[...] = jnp.where(spread == region.astype(F32), 1.0, 0.0).astype(BF)
    for f in range(frames_here):
        tiles = jnp.concatenate(
            [piece[f * REGIONS : (f + 1) * REGIONS, :] for piece in pieces], axis=0
        )
        summed[f * places : (f + 1) * places, :] = jnp.dot(
            picks[f * places : (f + 1) * places, :], tiles, preferred_element_type=F32
        )
    for s in range(SUBJ_DEV):
        tokens = jnp.concatenate(
            [
                summed[pl.ds(s * parts + p, frames_here, stride=places), :]
                for p in range(parts)
            ],
            axis=1,
        )
        tokens_ref[s * frames_here : (s + 1) * frames_here, :] = tokens
        power = jnp.mean(tokens * tokens, axis=1, keepdims=True)
        normed_ref[s * frames_here : (s + 1) * frames_here, :] = (
            tokens * lax.rsqrt(power + EPS)
        ).astype(BF)


def build_tokens(pieces, parts, frames_here):
    cams = len(pieces)
    rows = SUBJ_DEV * frames_here
    width = parts * LANES
    places = SUBJ_DEV * parts
    me = lax.axis_index("cam").astype(jnp.int32).reshape(1)
    return pl.pallas_call(
        functools.partial(token_kernel, cams=cams, parts=parts, frames_here=frames_here),
        out_shape=(
            jax.ShapeDtypeStruct((rows, width), F32),
            jax.ShapeDtypeStruct((rows, width), BF),
        ),
        in_specs=[pl.BlockSpec(memory_space=pltpu.SMEM)] + [VMEM_ALL] * cams,
        out_specs=(VMEM_ALL, VMEM_ALL),
        scratch_shapes=[
            pltpu.VMEM((cams * frames_here, LANES), F32),
            pltpu.VMEM((frames_here * places, cams), BF),
            pltpu.VMEM((frames_here * places, cams * REGIONS), BF),
            pltpu.VMEM((frames_here * places, LANES), F32),
        ],
        compiler_params=pltpu.CompilerParams(vmem_limit_bytes=50 << 20),
    )(me, *pieces)


def attention_kernel(
    mixed_ref, other_ref, key_w_ref, value_w_ref, out_w_ref, bias_ref, tokens_ref,
    out_ref, other_keys, other_values, attended, *, frames_here
):
    rows, width = tokens_ref.shape
    others = other_ref.shape[0] // rows
    head_size = width // HEADS
    scale = 1.0 / math.sqrt(head_size)
    other_keys[...] = jnp.dot(
        other_ref[...], key_w_ref[...], preferred_element_type=F32
    ).astype(BF)
    other_values[...] = jnp.dot(
        other_ref[...], value_w_ref[...], preferred_element_type=F32
    ).astype(BF)
    span = (others + 1) * frames_here
    heads = LANES // head_size
    head_of = lax.broadcasted_iota(jnp.int32, (frames_here, LANES), 1) // head_size
    for n in range(SUBJ_DEV):
        at = n * frames_here
        for tile in range(width // LANES):
            lanes = slice(tile * LANES, (tile + 1) * LANES)

            def gathered(own, rest):
                return jnp.concatenate(
                    [mixed_ref[at : at + frames_here, own + tile * LANES : own + (tile + 1) * LANES]]
                    + [
                        rest[k * rows + at : k * rows + at + frames_here, lanes]
                        for k in range(others)
                    ],
                    axis=0,
                )

            query = mixed_ref[at : at + frames_here, lanes]
            queries = jnp.concatenate(
                [jnp.where(head_of == h, query, jnp.zeros((), BF)) for h in range(heads)], axis=0
            )
            scores = lax.dot_general(
                queries,
                gathered(width, other_keys),
                (((1,), (1,)), ((), ())),
                preferred_element_type=F32,
            )
            bias = jnp.concatenate(
                [
                    jnp.broadcast_to(
                        bias_ref[n, tile * heads + h : tile * heads + h + 1, :],
                        (frames_here, span),
                    )
                    for h in range(heads)
                ],
                axis=0,
            )
            scores = scores * scale + bias
            weights = jnp.exp(scores - jnp.max(scores, axis=1, keepdims=True))
            denominator = jnp.sum(weights, axis=1, keepdims=True)
            numerator = jnp.dot(
                weights.astype(BF), gathered(2 * width, other_values), preferred_element_type=F32
            )
            ratio = numerator / denominator
            result = ratio[:frames_here]
            for h in range(1, heads):
                result = jnp.where(
                    head_of == h, ratio[h * frames_here : (h + 1) * frames_here], result
                )
            attended[at : at + frames_here, lanes] = result.astype(BF)
    out_ref[...] = (
        tokens_ref[...] + jnp.dot(attended[...], out_w_ref[...], preferred_element_type=F32)
    ).astype(BF)


def attend(mixed, other, qkv_w, out_w, bias, tokens, frames_here):
    rows, width = tokens.shape
    whole = lambda array: pl.BlockSpec(array.shape, lambda i: (0,) * array.ndim)
    return pl.pallas_call(
        functools.partial(attention_kernel, frames_here=frames_here),
        grid=(1,),
        out_shape=jax.ShapeDtypeStruct((rows, width), BF),
        in_specs=[
            whole(mixed),
            whole(other),
            pl.BlockSpec((width, width), lambda i: (0, 1)),
            pl.BlockSpec((width, width), lambda i: (0, 2)),
            whole(out_w),
            whole(bias),
            whole(tokens),
        ],
        out_specs=whole(tokens),
        scratch_shapes=[
            pltpu.VMEM(other.shape, BF),
            pltpu.VMEM(other.shape, BF),
            pltpu.VMEM((rows, width), BF),
        ],
        compiler_params=pltpu.CompilerParams(vmem_limit_bytes=56 << 20),
    )(mixed, other, qkv_w, qkv_w, out_w, bias, tokens)


def per_device(
    frames, conv1_w, conv2_w, tile_w, vis_subject, part_count, part_region, subject_slot,
    qkv_w, out_w, key_bias
):
    frames_here = frames.shape[1]
    parts = part_region.shape[3]
    payload = camera_tiles(
        frames, conv1_w, conv2_w, tile_w, vis_subject, part_count, part_region, subject_slot
    )
    tokens, normed = build_tokens(exchange(payload), parts, frames_here)
    splits = lax.axis_size("frame")
    others = [
        lax.ppermute(normed, "frame", [((i + k) % splits, i) for i in range(splits)])
        for k in range(1, splits)
    ]
    other = others[0] if splits == 2 else jnp.concatenate(others, axis=0)
    mixed = jnp.dot(normed, qkv_w, preferred_element_type=F32).astype(BF)
    span = key_bias.shape[2]
    bias = lax.dynamic_slice_in_dim(
        jnp.concatenate([key_bias, key_bias], axis=2),
        lax.axis_index("frame") * frames_here,
        span,
        axis=2,
    )
    posed = attend(mixed, other, qkv_w, out_w, bias, tokens, frames_here)
    return posed.reshape(SUBJ_DEV, frames_here, tokens.shape[1])


def solution(mesh):
    in_specs = (
        P("cam", "frame", None, None),
        P(),
        P(),
        P(),
        P("cam", "frame", None),
        P("cam", "frame", None),
        P("cam", "frame", None, None),
        P(),
        P(),
        P(),
        P("cam", None, None),
    )
    out_specs = P("cam", "frame", None)
    return jax.shard_map(
        per_device, mesh=mesh, in_specs=in_specs, out_specs=out_specs, check_vma=False
    )
```

time: 142 us -> 75 us (0.53)
  the two profiles are of different devices: /device:TPU:12 before, /device:TPU:10 now
where the time goes in v1:
time: 75 us; the launch traced here: 74.4 us
  Pallas kernels  23.2 us (31%)
  waiting for transfers between devices  22.3 us (30%)
  starting transfers between devices  13.1 us (17%)
  local copies, waits for them, and re-layouts  9.54 us (13%)
  matrix products  4.66 us (6%)
  other arithmetic  1.54 us (2%)
    ppermute x15, waiting for transfers between devices, swap(): return lax.ppermute(array, 'cam', [(i, i ^ bits) for i in range(cams)])  18.9 us
    ppermute x15, starting transfers between devices, swap(): return lax.ppermute(array, 'cam', [(i, i ^ bits) for i in range(cams)])  12.6 us
    pallas_call x1, Pallas kernels, attend(): pl.pallas_call(functools.partial(attention_kernel, frames_here=frames_her...  11.9 us
    pallas_call x1, Pallas kernels, camera_tiles(): pl.pallas_call(functools.partial(camera_kernel, subjects=slots.shape[0],...  9.97 us
    unnamed x18, local copies, waits for them, and re-layouts  7.96 us
    dot_general x1, matrix products, per_device(): mixed = jnp.dot(normed, qkv_w, preferred_element_type=F32).astype(BF)  4.66 us
    ppermute x1, waiting for transfers between devices, per_device(): lax.ppermute(normed, 'frame', [((i + k) % splits, i) for i in range(split...  3.36 us
    concatenate x1, other arithmetic, per_device(): jnp.concatenate([key_bias, key_bias], axis=2)  1.54 us
  transfers between devices with their start and end apart: 16, of which 6 were waited for; matrix products, arithmetic and copies ran while one was open for 8% of the time, Pallas kernels for 0%

profile of v1, /device:TPU:10, one launch (start us, length us, event | category | flops | bytes accessed | tf_op | source)
XLA Modules:
  0.0 74.4 jit_solution(12256363003696510919)
XLA Ops:
  0.0 0.8 %copy.17 = s32[1,32,12]{2,1,0:T(8,128)S(1)} copy(s32[1,32,12]{1,0,2:T(1,128)} %param.17) | data formatting | bytes 3072 | tf_op args[4]
  0.8 0.8 %copy.18 = s32[1,32,12]{2,1,0:T(8,128)S(1)} copy(s32[1,32,12]{1,0,2:T(1,128)} %param.18) | data formatting | bytes 3072 | tf_op args[5]
  1.5 0.9 %copy.19.region_ref = s32[32,96]{1,0:T(8,128)S(1)} copy(s32[32,96]{0,1:T(8,128)} %bitcast.13) | data formatting | bytes 24576 | tf_op jit(solution)/shard_map/reshape;squeeze | solution.py:184
  2.4 0.7 pad.4.w1_ref
  3.1 1.1 %copy-done = bf16[1,32,3,4096]{3,1,2,0:T(8,128)(2,1)S(1)} copy-done((bf16[1,32,3,4096]{3,1,2,0:T(8,128)(2,1)S(1)}, bf16[1,32,3,4096]{3,1,2,0:T(8,128)(2,1)}, u32[]{:S(2)}) %copy-start) | copy-done | bytes 786456
  4.3 1.1 %copy-done.1 = bf16[1152,256]{1,0:T(8,128)(2,1)S(1)} copy-done((bf16[1152,256]{1,0:T(8,128)(2,1)S(1)}, bf16[1152,256]{1,0:T(8,128)(2,1)}, u32[]{:S(2)}) %copy-start.1) | copy-done | bytes 589848
  5.3 1.0 %copy-done.3 = bf16[2048,32]{1,0:T(8,128)(2,1)S(1)} copy-done((bf16[2048,32]{1,0:T(8,128)(2,1)S(1)}, bf16[2048,32]{1,0:T(8,128)(2,1)}, u32[]{:S(2)}) %copy-start.3) | copy-done | bytes 131096
  6.4 1.0 %copy-done.4 = bf16[384,512]{1,0:T(8,128)(2,1)S(1)} copy-done((bf16[384,512]{1,0:T(8,128)(2,1)S(1)}, bf16[384,512]{1,0:T(8,128)(2,1)}, u32[]{:S(2)}) %copy-start.4) | copy-done | bytes 393240
  7.4 0.8 %copy-done.5 = bf16[256,128]{1,0:T(8,128)(2,1)S(1)} copy-done((bf16[256,128]{1,0:T(8,128)(2,1)S(1)}, bf16[256,128]{1,0:T(8,128)(2,1)}, u32[]{:S(2)}) %copy-start.5) | copy-done | bytes 65560
  8.2 0.7 copy-done.6
  8.8 10.0 %shard_map.127.refs_0_ = bf16[576,128]{1,0:T(8,128)(2,1)S(1)} custom-call(bf16[3,32,4096]{2,1,0:T(8,128)(2,1)S(1)} %bitcast.10, bf16[384,512]{1,0:T(8,128)(2,1)S(1)} %copy-done.4, bf16[2048,32]{1,0:T(8,128)(2,1)S(1)} %copy-done.3, bf16[32,128]{1,0:T(8,128)(2,1)S(1)} %pad.4.w1_ref, bf16[1152,256]{1,0:T(8,128)(2,1)S(1)} %copy-done.1, ...), custom_call_target="tpu_custom_call" | custom-call | tf_op jit(solution)/shard_map/pallas_call | solution.py:163
  18.8 1.5 %collective-permute-start.2 = (bf16[576,128]{1,0:T(8,128)(2,1)S(1)}, bf16[576,128]{1,0:T(8,128)(2,1)S(1)}, u32[]{:S(2)}, u32[]{:S(2)}) collective-permute-start(bf16[576,128]{1,0:T(8,128)(2,1)S(1)} %shard_map.127.refs_0_), channel_id=1, source_target_pairs={{0,12},{2,14},{4,8},{6,10},{8,4},{10,6},{12,0},{14,2},{16,28},{18,... | collective-permute-start | bytes 442376 | tf_op jit(solution)/shard_map/ppermute | solution.py:196
  20.3 2.6 %collective-permute-start.3 = (bf16[576,128]{1,0:T(8,128)(2,1)S(1)}, bf16[576,128]{1,0:T(8,128)(2,1)S(1)}, u32[]{:S(2)}, u32[]{:S(2)}) collective-permute-start(bf16[576,128]{1,0:T(8,128)(2,1)S(1)} %shard_map.127.refs_0_), channel_id=1, source_target_pairs={{0,16},{2,18},{4,20},{6,22},{8,24},{10,26},{12,28},{14,30},{16,0},... | collective-permute-start | bytes 442376 | tf_op jit(solution)/shard_map/ppermute | solution.py:196
  22.9 0.3 collective-permute-start.4
  23.2 2.7 %collective-permute-start.5 = (bf16[576,128]{1,0:T(8,128)(2,1)S(1)}, bf16[576,128]{1,0:T(8,128)(2,1)S(1)}, u32[]{:S(2)}, u32[]{:S(2)}) collective-permute-start(bf16[576,128]{1,0:T(8,128)(2,1)S(1)} %shard_map.127.refs_0_), channel_id=1, source_target_pairs={{0,24},{2,26},{4,28},{6,30},{8,16},{10,18},{12,20},{14,22},{16,8},... | collective-permute-start | bytes 442376 | tf_op jit(solution)/shard_map/ppermute | solution.py:196
  25.9 1.0 %collective-permute-start.6 = (bf16[576,128]{1,0:T(8,128)(2,1)S(1)}, bf16[576,128]{1,0:T(8,128)(2,1)S(1)}, u32[]{:S(2)}, u32[]{:S(2)}) collective-permute-start(bf16[576,128]{1,0:T(8,128)(2,1)S(1)} %shard_map.127.refs_0_), channel_id=1, source_target_pairs={{0,28},{2,30},{4,24},{6,26},{8,20},{10,22},{12,16},{14,18},{16,12}... | collective-permute-start | bytes 442376 | tf_op jit(solution)/shard_map/ppermute | solution.py:196
  26.8 0.0 collective-permute-done.2.refs_3_
  26.8 0.9 %collective-permute-start = (bf16[576,128]{1,0:T(8,128)(2,1)S(1)}, bf16[576,128]{1,0:T(8,128)(2,1)S(1)}, u32[]{:S(2)}, u32[]{:S(2)}) collective-permute-start(bf16[576,128]{1,0:T(8,128)(2,1)S(1)} %shard_map.127.refs_0_), channel_id=1, source_target_pairs={{0,4},{2,6},{4,0},{6,2},{8,12},{10,14},{12,8},{14,10},{16,20},{18,... | collective-permute-start | bytes 442376 | tf_op jit(solution)/shard_map/ppermute | solution.py:196
  27.8 11.8 %collective-permute-done.3.refs_4_ = bf16[576,128]{1,0:T(8,128)(2,1)S(1)} collective-permute-done((bf16[576,128]{1,0:T(8,128)(2,1)S(1)}, bf16[576,128]{1,0:T(8,128)(2,1)S(1)}, u32[]{:S(2)}, u32[]{:S(2)}) %collective-permute-start.3) | collective-permute-done | bytes 147488 | tf_op jit(solution)/shard_map/ppermute | solution.py:196
  39.6 2.4 %collective-permute-start.1 = (bf16[576,128]{1,0:T(8,128)(2,1)S(1)}, bf16[576,128]{1,0:T(8,128)(2,1)S(1)}, u32[]{:S(2)}, u32[]{:S(2)}) collective-permute-start(bf16[576,128]{1,0:T(8,128)(2,1)S(1)} %shard_map.127.refs_0_), channel_id=1, source_target_pairs={{0,8},{2,10},{4,12},{6,14},{8,0},{10,2},{12,4},{14,6},{16,24},{18,... | collective-permute-start | bytes 442376 | tf_op jit(solution)/shard_map/ppermute | solution.py:196
  41.9 0.8 %collective-permute-done.4.refs_5_ = bf16[576,128]{1,0:T(8,128)(2,1)S(1)} collective-permute-done((bf16[576,128]{1,0:T(8,128)(2,1)S(1)}, bf16[576,128]{1,0:T(8,128)(2,1)S(1)}, u32[]{:S(2)}, u32[]{:S(2)}) %collective-permute-start.4) | collective-permute-done | bytes 147488 | tf_op jit(solution)/shard_map/ppermute | solution.py:196
  42.7 0.0 collective-permute-start.7
  42.7 4.1 %collective-permute-done.5.refs_6_ = bf16[576,128]{1,0:T(8,128)(2,1)S(1)} collective-permute-done((bf16[576,128]{1,0:T(8,128)(2,1)S(1)}, bf16[576,128]{1,0:T(8,128)(2,1)S(1)}, u32[]{:S(2)}, u32[]{:S(2)}) %collective-permute-start.5) | collective-permute-done | bytes 147488 | tf_op jit(solution)/shard_map/ppermute | solution.py:196
  46.8 0.0 collective-permute-start.10
  46.8 1.9 %collective-permute-done.6.refs_7_ = bf16[576,128]{1,0:T(8,128)(2,1)S(1)} collective-permute-done((bf16[576,128]{1,0:T(8,128)(2,1)S(1)}, bf16[576,128]{1,0:T(8,128)(2,1)S(1)}, u32[]{:S(2)}, u32[]{:S(2)}) %collective-permute-start.6) | collective-permute-done | bytes 147488 | tf_op jit(solution)/shard_map/ppermute | solution.py:196
  48.7 0.0 collective-permute-start.11
  48.7 0.0 collective-permute-done.refs_1_
  48.7 0.5 collective-permute-start.12
  49.2 0.0 collective-permute-done.1.refs_2_
  49.2 0.1 collective-permute-start.13
  49.3 0.0 collective-permute-done.7.refs_8_
  49.3 0.4 collective-permute-start.14
  49.8 0.0 collective-permute-done.10.refs_11_
  49.8 0.1 collective-permute-start.8
  49.8 0.3 collective-permute-done.11.refs_12_
  50.1 0.2 collective-permute-start.9
  50.3 1.5 %dynamic-slice_maximum_fusion.bias_ref = f32[4,16,64]{2,1,0:T(8,128)} fusion(s32[]{:T(128)S(6)} %select_n.3, f32[4,16,64]{2,1,0:T(8,128)} %param.23), kind=kLoop, calls=%fused_computation.1 | loop fusion | flops 4096 | bytes 32772 | tf_op jit(solution)/shard_map/concatenate | solution.py:413
  51.8 0.0 collective-permute-done.12.refs_13_
  51.8 0.0 collective-permute-done.13.refs_14_
  51.8 0.0 collective-permute-done.14.refs_15_
  51.8 0.0 collective-permute-done.8.refs_9_
  51.8 0.0 collective-permute-done.9.refs_10_
  51.9 1.4 %shard_map.128 = (f32[128,1024]{1,0:T(8,128)S(1)}, bf16[128,1024]{1,0:T(8,128)(2,1)S(1)}) custom-call(s32[1]{0:T(128)} %bitcast.me_ref, bf16[576,128]{1,0:T(8,128)(2,1)S(1)} %shard_map.127.refs_0_, bf16[576,128]{1,0:T(8,128)(2,1)S(1)} %collective-permute-done.refs_1_, bf16[576,128]{1,0:T(8,128)(2,1)S(1)} %collective-permute-done.1.refs_2_, ...), custom_call_target="tpu_custom_call" | custom-call | tf_op jit(solution)/shard_map/pallas_call | solution.py:280
  53.3 0.6 collective-permute-start.15
  53.9 4.7 %convolution_convert_fusion.mixed_ref = bf16[128,3072]{1,0:T(8,128)(2,1)} fusion(bf16[128,1024]{1,0:T(8,128)(2,1)S(1)} %get-tuple-element.7, bf16[1024,3072]{1,0:T(8,128)(2,1)} %value_w_ref.1), kind=kOutput, calls=%fused_computation | convolution fusion | flops 805699584 | bytes 7340032 | tf_op jit(solution)/shard_map/dot_general | solution.py:410
  58.5 3.4 %collective-permute-done.15.other_ref = bf16[128,1024]{1,0:T(8,128)(2,1)S(1)} collective-permute-done((bf16[128,1024]{1,0:T(8,128)(2,1)S(1)}, bf16[128,1024]{1,0:T(8,128)(2,1)S(1)}, u32[]{:S(2)}, u32[]{:S(2)}) %collective-permute-start.15) | collective-permute-done | bytes 262176 | tf_op jit(solution)/shard_map/ppermute | solution.py:406
  61.9 0.7 copy-done.7
  62.6 11.9 %shard_map.129 = bf16[128,1024]{1,0:T(8,128)(2,1)} custom-call(bf16[128,3072]{1,0:T(8,128)(2,1)} %convolution_convert_fusion.mixed_ref, bf16[128,1024]{1,0:T(8,128)(2,1)} %copy-done.7, bf16[1024,3072]{1,0:T(8,128)(2,1)} %value_w_ref.1, bf16[1024,3072]{1,0:T(8,128)(2,1)} %value_w_ref.1, bf16[1024,1024]{1,0:T(8,128)(2,1)} %out_w_ref.1, ...), custom_call_target="tpu_custom_call" | custom-call | tf_op jit(solution)/shard_map/pallas_call | solution.py:371
  (9 shorter events, 0.0 us)
Async XLA Ops:
  3.1 1.1 %copy-start = (bf16[1,32,3,4096]{3,1,2,0:T(8,128)(2,1)S(1)}, bf16[1,32,3,4096]{3,1,2,0:T(8,128)(2,1)}, u32[]{:S(2)}) copy-start(bf16[1,32,3,4096]{3,1,2,0:T(8,128)(2,1)} %param.13) | copy-start | bytes 2359300
  4.3 1.1 %copy-start.1 = (bf16[1152,256]{1,0:T(8,128)(2,1)S(1)}, bf16[1152,256]{1,0:T(8,128)(2,1)}, u32[]{:S(2)}) copy-start(bf16[1152,256]{1,0:T(8,128)(2,1)} %w2_ref.1) | copy-start | bytes 1769476
  5.3 1.0 %copy-start.3 = (bf16[2048,32]{1,0:T(8,128)(2,1)S(1)}, bf16[2048,32]{1,0:T(8,128)(2,1)}, u32[]{:S(2)}) copy-start(bf16[2048,32]{1,0:T(8,128)(2,1)} %constant.21.clone.tap_ref) | copy-start | bytes 393220
  6.4 1.0 %copy-start.4 = (bf16[384,512]{1,0:T(8,128)(2,1)S(1)}, bf16[384,512]{1,0:T(8,128)(2,1)}, u32[]{:S(2)}) copy-start(bf16[384,512]{1,0:T(8,128)(2,1)} %constant.20.clone.pack_ref) | copy-start | bytes 1179652
  7.4 0.8 %copy-start.5 = (bf16[256,128]{1,0:T(8,128)(2,1)S(1)}, bf16[256,128]{1,0:T(8,128)(2,1)}, u32[]{:S(2)}) copy-start(bf16[256,128]{1,0:T(8,128)(2,1)} %wt_ref.1) | copy-start | bytes 196612
  8.2 0.7 copy-start.6
  18.8 8.0 %collective-permute-start.2 = (bf16[576,128]{1,0:T(8,128)(2,1)S(1)}, bf16[576,128]{1,0:T(8,128)(2,1)S(1)}, u32[]{:S(2)}, u32[]{:S(2)}) collective-permute-start(bf16[576,128]{1,0:T(8,128)(2,1)S(1)} %shard_map.127.refs_0_), channel_id=1, source_target_pairs={{0,12},{2,14},{4,8},{6,10},{8,4},{10,6},{12,0},{14,2},{16,28},{18,... | collective-permute-start | bytes 442376 | tf_op jit(solution)/shard_map/ppermute | solution.py:196
  20.3 19.3 %collective-permute-start.3 = (bf16[576,128]{1,0:T(8,128)(2,1)S(1)}, bf16[576,128]{1,0:T(8,128)(2,1)S(1)}, u32[]{:S(2)}, u32[]{:S(2)}) collective-permute-start(bf16[576,128]{1,0:T(8,128)(2,1)S(1)} %shard_map.127.refs_0_), channel_id=1, source_target_pairs={{0,16},{2,18},{4,20},{6,22},{8,24},{10,26},{12,28},{14,30},{16,0},... | collective-permute-start | bytes 442376 | tf_op jit(solution)/shard_map/ppermute | solution.py:196
  22.9 19.8 %collective-permute-start.4 = (bf16[576,128]{1,0:T(8,128)(2,1)S(1)}, bf16[576,128]{1,0:T(8,128)(2,1)S(1)}, u32[]{:S(2)}, u32[]{:S(2)}) collective-permute-start(bf16[576,128]{1,0:T(8,128)(2,1)S(1)} %shard_map.127.refs_0_), channel_id=1, source_target_pairs={{0,20},{2,22},{4,16},{6,18},{8,28},{10,30},{12,24},{14,26},{16,4},... | collective-permute-start | bytes 442376 | tf_op jit(solution)/shard_map/ppermute | solution.py:196
  23.2 23.6 %collective-permute-start.5 = (bf16[576,128]{1,0:T(8,128)(2,1)S(1)}, bf16[576,128]{1,0:T(8,128)(2,1)S(1)}, u32[]{:S(2)}, u32[]{:S(2)}) collective-permute-start(bf16[576,128]{1,0:T(8,128)(2,1)S(1)} %shard_map.127.refs_0_), channel_id=1, source_target_pairs={{0,24},{2,26},{4,28},{6,30},{8,16},{10,18},{12,20},{14,22},{16,8},... | collective-permute-start | bytes 442376 | tf_op jit(solution)/shard_map/ppermute | solution.py:196
  25.9 22.9 %collective-permute-start.6 = (bf16[576,128]{1,0:T(8,128)(2,1)S(1)}, bf16[576,128]{1,0:T(8,128)(2,1)S(1)}, u32[]{:S(2)}, u32[]{:S(2)}) collective-permute-start(bf16[576,128]{1,0:T(8,128)(2,1)S(1)} %shard_map.127.refs_0_), channel_id=1, source_target_pairs={{0,28},{2,30},{4,24},{6,26},{8,20},{10,22},{12,16},{14,18},{16,12}... | collective-permute-start | bytes 442376 | tf_op jit(solution)/shard_map/ppermute | solution.py:196
  26.8 21.9 %collective-permute-start = (bf16[576,128]{1,0:T(8,128)(2,1)S(1)}, bf16[576,128]{1,0:T(8,128)(2,1)S(1)}, u32[]{:S(2)}, u32[]{:S(2)}) collective-permute-start(bf16[576,128]{1,0:T(8,128)(2,1)S(1)} %shard_map.127.refs_0_), channel_id=1, source_target_pairs={{0,4},{2,6},{4,0},{6,2},{8,12},{10,14},{12,8},{14,10},{16,20},{18,... | collective-permute-start | bytes 442376 | tf_op jit(solution)/shard_map/ppermute | solution.py:196
  39.6 9.7 %collective-permute-start.1 = (bf16[576,128]{1,0:T(8,128)(2,1)S(1)}, bf16[576,128]{1,0:T(8,128)(2,1)S(1)}, u32[]{:S(2)}, u32[]{:S(2)}) collective-permute-start(bf16[576,128]{1,0:T(8,128)(2,1)S(1)} %shard_map.127.refs_0_), channel_id=1, source_target_pairs={{0,8},{2,10},{4,12},{6,14},{8,0},{10,2},{12,4},{14,6},{16,24},{18,... | collective-permute-start | bytes 442376 | tf_op jit(solution)/shard_map/ppermute | solution.py:196
  42.7 6.6 %collective-permute-start.7 = (bf16[576,128]{1,0:T(8,128)(2,1)S(1)}, bf16[576,128]{1,0:T(8,128)(2,1)S(1)}, u32[]{:S(2)}, u32[]{:S(2)}) collective-permute-start(bf16[576,128]{1,0:T(8,128)(2,1)S(1)} %shard_map.127.refs_0_), channel_id=1, source_target_pairs={{0,2},{2,0},{4,6},{6,4},{8,10},{10,8},{12,14},{14,12},{16,18},{18,... | collective-permute-start | bytes 442376 | tf_op jit(solution)/shard_map/ppermute | solution.py:196
  46.8 3.0 %collective-permute-start.10 = (bf16[576,128]{1,0:T(8,128)(2,1)S(1)}, bf16[576,128]{1,0:T(8,128)(2,1)S(1)}, u32[]{:S(2)}, u32[]{:S(2)}) collective-permute-start(bf16[576,128]{1,0:T(8,128)(2,1)S(1)} %collective-permute-done.2.refs_3_), channel_id=1, source_target_pairs={{0,2},{2,0},{4,6},{6,4},{8,10},{10,8},{12,14},{14,12},{16,18},{18,... | collective-permute-start | bytes 442376 | tf_op jit(solution)/shard_map/ppermute | solution.py:196
  48.7 1.4 %collective-permute-start.11 = (bf16[576,128]{1,0:T(8,128)(2,1)S(1)}, bf16[576,128]{1,0:T(8,128)(2,1)S(1)}, u32[]{:S(2)}, u32[]{:S(2)}) collective-permute-start(bf16[576,128]{1,0:T(8,128)(2,1)S(1)} %collective-permute-done.3.refs_4_), channel_id=1, source_target_pairs={{0,2},{2,0},{4,6},{6,4},{8,10},{10,8},{12,14},{14,12},{16,18},{18,... | collective-permute-start | bytes 442376 | tf_op jit(solution)/shard_map/ppermute | solution.py:196
  48.7 3.1 %collective-permute-start.12 = (bf16[576,128]{1,0:T(8,128)(2,1)S(1)}, bf16[576,128]{1,0:T(8,128)(2,1)S(1)}, u32[]{:S(2)}, u32[]{:S(2)}) collective-permute-start(bf16[576,128]{1,0:T(8,128)(2,1)S(1)} %collective-permute-done.4.refs_5_), channel_id=1, source_target_pairs={{0,2},{2,0},{4,6},{6,4},{8,10},{10,8},{12,14},{14,12},{16,18},{18,... | collective-permute-start | bytes 442376 | tf_op jit(solution)/shard_map/ppermute | solution.py:196
  49.2 2.6 %collective-permute-start.13 = (bf16[576,128]{1,0:T(8,128)(2,1)S(1)}, bf16[576,128]{1,0:T(8,128)(2,1)S(1)}, u32[]{:S(2)}, u32[]{:S(2)}) collective-permute-start(bf16[576,128]{1,0:T(8,128)(2,1)S(1)} %collective-permute-done.5.refs_6_), channel_id=1, source_target_pairs={{0,2},{2,0},{4,6},{6,4},{8,10},{10,8},{12,14},{14,12},{16,18},{18,... | collective-permute-start | bytes 442376 | tf_op jit(solution)/shard_map/ppermute | solution.py:196
  49.3 2.5 %collective-permute-start.14 = (bf16[576,128]{1,0:T(8,128)(2,1)S(1)}, bf16[576,128]{1,0:T(8,128)(2,1)S(1)}, u32[]{:S(2)}, u32[]{:S(2)}) collective-permute-start(bf16[576,128]{1,0:T(8,128)(2,1)S(1)} %collective-permute-done.6.refs_7_), channel_id=1, source_target_pairs={{0,2},{2,0},{4,6},{6,4},{8,10},{10,8},{12,14},{14,12},{16,18},{18,... | collective-permute-start | bytes 442376 | tf_op jit(solution)/shard_map/ppermute | solution.py:196
  49.8 2.1 %collective-permute-start.8 = (bf16[576,128]{1,0:T(8,128)(2,1)S(1)}, bf16[576,128]{1,0:T(8,128)(2,1)S(1)}, u32[]{:S(2)}, u32[]{:S(2)}) collective-permute-start(bf16[576,128]{1,0:T(8,128)(2,1)S(1)} %collective-permute-done.refs_1_), channel_id=1, source_target_pairs={{0,2},{2,0},{4,6},{6,4},{8,10},{10,8},{12,14},{14,12},{16,18},{18,... | collective-permute-start | bytes 442376 | tf_op jit(solution)/shard_map/ppermute | solution.py:196
  50.1 1.7 %collective-permute-start.9 = (bf16[576,128]{1,0:T(8,128)(2,1)S(1)}, bf16[576,128]{1,0:T(8,128)(2,1)S(1)}, u32[]{:S(2)}, u32[]{:S(2)}) collective-permute-start(bf16[576,128]{1,0:T(8,128)(2,1)S(1)} %collective-permute-done.1.refs_2_), channel_id=1, source_target_pairs={{0,2},{2,0},{4,6},{6,4},{8,10},{10,8},{12,14},{14,12},{16,18},{18,... | collective-permute-start | bytes 442376 | tf_op jit(solution)/shard_map/ppermute | solution.py:196
  53.3 8.6 %copy-start.2 = (f32[128,1024]{1,0:T(8,128)}, f32[128,1024]{1,0:T(8,128)S(1)}, u32[]{:S(2)}) copy-start(f32[128,1024]{1,0:T(8,128)S(1)} %get-tuple-element.8.tokens_ref) | copy-start | bytes 1572868
  53.3 8.6 %collective-permute-start.15 = (bf16[128,1024]{1,0:T(8,128)(2,1)S(1)}, bf16[128,1024]{1,0:T(8,128)(2,1)S(1)}, u32[]{:S(2)}, u32[]{:S(2)}) collective-permute-start(bf16[128,1024]{1,0:T(8,128)(2,1)S(1)} %get-tuple-element.7), channel_id=1, source_target_pairs={{1,0},{0,1},{3,2},{2,3},{5,4},{4,5},{7,6},{6,7},{9,8},{8,9},{11,10... | collective-permute-start | bytes 786440 | tf_op jit(solution)/shard_map/ppermute | solution.py:406
  61.9 0.7 copy-start.7

commit v2 on v1

--- a/solution.py
+++ b/solution.py
@@ -42,7 +42,7 @@
 
 
 def tap_table():
-    table = np.zeros((GROUP, 2 * LANES, 32), np.float32)
+    table = np.zeros((GROUP, 2 * LANES, 27), np.float32)
     for column in range(GROUP):
         for dy in range(3):
             base = {1: 0, 2: IMG, 0: LANES + IMG}[dy]
@@ -50,53 +50,72 @@
                 for ch in range(3):
                     lane = base + ch * SEG + 2 * column + dx
                     table[column, lane, dy * 9 + dx * 3 + ch] = 1.0
-    return table.reshape(GROUP * 2 * LANES, 32)
+    return table.reshape(GROUP * 2 * LANES, 27)
 
 
 def camera_kernel(
-    x_ref, pack_ref, tap_ref, w1_ref, w2_ref, wt_ref, vis_ref, count_ref, region_ref, slot_ref,
-    out_ref, packed, wide, cells, part, *, subjects, parts
+    x_hbm, pack_hbm, tap_hbm, w1_hbm, w2_hbm, wt_hbm, vis_hbm, count_hbm, region_hbm, slot_hbm,
+    out_ref, x_ref, pack_ref, tap_ref, w1_ref, w2_ref, wt_ref, vis_ref, count_ref, region_ref,
+    slot_ref, sems, packed, wide, cells, part, *, subjects, parts
 ):
+    sources = (
+        slot_hbm, vis_hbm, count_hbm, region_hbm, w1_hbm, tap_hbm, pack_hbm, x_hbm, w2_hbm, wt_hbm
+    )
+    targets = (
+        slot_ref, vis_ref, count_ref, region_ref, w1_ref, tap_ref, pack_ref, x_ref, w2_ref, wt_ref
+    )
+    copies = [
+        pltpu.make_async_copy(source, target, sems.at[k])
+        for k, (source, target) in enumerate(zip(sources, targets))
+    ]
+    for copy in copies:
+        copy.start()
     frames_here = x_ref.shape[1]
     rows = OUT1 * frames_here
-    listed = vis_ref.shape[1]
+    listed = vis_ref.shape[0]
     lanes = listed * parts
     expand = (
-        lax.broadcasted_iota(jnp.int32, (listed, lanes), 1) // parts
-        == lax.broadcasted_iota(jnp.int32, (listed, lanes), 0)
+        lax.broadcasted_iota(jnp.int32, (lanes, listed), 0) // parts
+        == lax.broadcasted_iota(jnp.int32, (lanes, listed), 1)
     ).astype(BF)
-
-    def spread(ref):
-        return jnp.dot(ref[...].astype(F32).astype(BF), expand, preferred_element_type=F32)
-
-    who = spread(vis_ref).astype(jnp.int32)
-    count = spread(count_ref).astype(jnp.int32)
-    part_of = lax.broadcasted_iota(jnp.int32, (frames_here, lanes), 1) % parts
-    code = jnp.where(part_of < count, region_ref[...] + 1, 0)
-    row_of = jnp.zeros((frames_here, lanes), jnp.int32)
-    for subject in range(subjects):
-        row_of = jnp.where(who == subject, slot_ref[subject], row_of)
-    blocks = -(-lanes // LANES)
-    fill = blocks * LANES - lanes
-    if fill:
-        zeros = jnp.zeros((frames_here, fill), jnp.int32)
-        code = jnp.concatenate([code, zeros], axis=1)
-        row_of = jnp.concatenate([row_of, zeros], axis=1)
-    base = REGIONS * frames_here
-    for k, array in enumerate((code, row_of)):
-        for block in range(blocks):
-            at = base + (k * blocks + block) * frames_here
-            out_ref[at : at + frames_here, :] = (
-                array[:, block * LANES : (block + 1) * LANES].astype(F32).astype(BF)
-            )
-
+    part_of = lax.broadcasted_iota(jnp.int32, (lanes, frames_here), 0) % parts
+
+    for copy in copies[:6]:
+        copy.wait()
     for column in range(GROUP):
         wide[:, column * LANES : (column + 1) * LANES] = jnp.dot(
             tap_ref[column * 2 * LANES : (column + 1) * 2 * LANES, :],
             w1_ref[...],
             preferred_element_type=F32,
         ).astype(BF)
+
+    def spread(ref):
+        return jnp.dot(
+            expand, ref[:, 0, :].astype(F32).astype(BF), preferred_element_type=F32
+        ).astype(jnp.int32)
+
+    who = spread(vis_ref)
+    code = jnp.where(part_of < spread(count_ref), region_ref[...] + 1, 0)
+    row_of = jnp.zeros((lanes, frames_here), jnp.int32)
+    for subject in range(subjects):
+        row_of = jnp.where(who == subject, slot_ref[subject], row_of)
+    blocks = -(-lanes // LANES)
+    fill = blocks * LANES - lanes
+    base = REGIONS * frames_here
+    for k, array in enumerate((code, row_of)):
+        array = array.astype(F32)
+        if fill:
+            array = jnp.concatenate([array, jnp.zeros((fill, frames_here), F32)], axis=0)
+        array = array.T.astype(BF)
+        for block in range(blocks):
+            at = base + (k * blocks + block) * frames_here
+            out_ref[at : at + frames_here, :] = array[:, block * LANES : (block + 1) * LANES]
+
+    cells[0] = jnp.zeros(cells.shape[1:], BF)
+    cells[:, 1, 0] = jnp.zeros((cells.shape[0],) + cells.shape[3:], BF)
     packed[:, 0:frames_here, :] = jnp.zeros((GROUPS, frames_here, LANES), BF)
+    copies[6].wait()
+    copies[7].wait()
     images = jnp.concatenate(
         [
             jnp.concatenate(
@@ -110,8 +129,6 @@
         packed[group, frames_here:, :] = jnp.dot(
             images, pack_ref[:, group * LANES : (group + 1) * LANES], preferred_element_type=F32
         ).astype(BF)
-    cells[0] = jnp.zeros(cells.shape[1:], BF)
-    cells[:, 1, 0] = jnp.zeros((cells.shape[0],) + cells.shape[3:], BF)
     for group in range(GROUPS):
         lhs = jnp.concatenate(
             [packed[group, frames_here:, :], packed[group, 0:rows, :]], axis=1
@@ -125,6 +142,8 @@
             cells[1:, 0, at] = both[:, :LANES].reshape(OUT1, frames_here, LANES)
             cells[1:, 1, at + 1] = both[:, LANES:].reshape(OUT1, frames_here, LANES)
 
+    copies[8].wait()
+    copies[9].wait()
     width = w2_ref.shape[1]
     for ry in range(RGRID):
         total = jnp.zeros((RGRID, frames_here, width), F32)
@@ -158,32 +177,34 @@
     frames_here = frames.shape[1]
     listed, parts = part_region.shape[2:]
     blocks = -(-listed * parts // LANES)
-    images = jnp.transpose(frames[0], (1, 0, 2))
-    taps = jnp.pad(conv1_w, ((0, 32 - conv1_w.shape[0]), (0, 0)))
+    operands = (
+        jnp.transpose(frames[0], (1, 0, 2)),
+        jnp.asarray(pack_table(), BF),
+        jnp.asarray(tap_table(), BF),
+        conv1_w,
+        conv2_w,
+        tile_w,
+        jnp.transpose(vis_subject, (2, 0, 1)),
+        jnp.transpose(part_count, (2, 0, 1)),
+        jnp.transpose(part_region[0], (1, 2, 0)).reshape(listed * parts, frames_here),
+        slots,
+    )
     return pl.pallas_call(
         functools.partial(camera_kernel, subjects=slots.shape[0], parts=parts),
         out_shape=jax.ShapeDtypeStruct(((REGIONS + 2 * blocks) * frames_here, LANES), BF),
-        in_specs=[VMEM_ALL] * 9 + [pl.BlockSpec(memory_space=pltpu.SMEM)],
+        in_specs=[pl.BlockSpec(memory_space=pltpu.HBM)] * len(operands),
         out_specs=VMEM_ALL,
-        scratch_shapes=[
+        scratch_shapes=[pltpu.VMEM(array.shape, array.dtype) for array in operands[:-1]]
+        + [
+            pltpu.SMEM(slots.shape, slots.dtype),
+            pltpu.SemaphoreType.DMA((len(operands),)),
             pltpu.VMEM((GROUPS, (OUT1 + 1) * frames_here, LANES), BF),
             pltpu.VMEM((2 * LANES, GROUP * LANES), BF),
             pltpu.VMEM((OUT1 + 1, 2, OUT2 + 1, frames_here, LANES), BF),
             pltpu.VMEM((REGIONS * frames_here, LANES), F32),
         ],
-        compiler_params=pltpu.CompilerParams(vmem_limit_bytes=50 << 20),
-    )(
-        images,
-        jnp.asarray(pack_table(), BF),
-        jnp.asarray(tap_table(), BF),
-        taps,
-        conv2_w,
-        tile_w,
-        vis_subject[0],
-        part_count[0],
-        part_region[0].reshape(frames_here, listed * parts),
-        slots,
-    )
+        compiler_params=pltpu.CompilerParams(vmem_limit_bytes=60 << 20),
+    )(*operands)
 
 
 def exchange(payload):
@@ -199,13 +220,15 @@
     return pieces + [swap(piece, 1) for piece in pieces]
 
 
-def token_kernel(me_ref, *refs, cams, parts, frames_here):
-    pieces = refs[:cams]
-    tokens_ref, normed_ref, marks, spots, picks, summed = refs[cams:]
+def token_kernel(*refs, cams, parts, frames_here):
+    tokens_ref, normed_ref, own, sem, marks, spots, picks, summed = refs[cams:]
+    copy = pltpu.make_async_copy(refs[0], own, sem)
+    copy.start()
+    pieces = refs[1:cams] + (own,)
     blocks = (pieces[0].shape[0] // frames_here - REGIONS) // 2
     lanes = blocks * LANES
     places = SUBJ_DEV * parts
-    first = me_ref[0] * SUBJ_DEV
+    first = lax.axis_index("cam") * SUBJ_DEV
     base = REGIONS * frames_here
     from_lane = lax.broadcasted_iota(jnp.int32, (SUBJ_DEV * lanes, LANES), 0)
     to_lane = lax.broadcasted_iota(jnp.int32, (SUBJ_DEV * lanes, LANES), 1)
@@ -214,6 +237,8 @@
     ).astype(BF)
     codes = []
     for piece in pieces:
+        if piece is own:
+            copy.wait()
 
         def field(k):
             return jnp.concatenate(
@@ -276,119 +301,193 @@
     rows = SUBJ_DEV * frames_here
     width = parts * LANES
     places = SUBJ_DEV * parts
-    me = lax.axis_index("cam").astype(jnp.int32).reshape(1)
     return pl.pallas_call(
         functools.partial(token_kernel, cams=cams, parts=parts, frames_here=frames_here),
         out_shape=(
             jax.ShapeDtypeStruct((rows, width), F32),
             jax.ShapeDtypeStruct((rows, width), BF),
         ),
-        in_specs=[pl.BlockSpec(memory_space=pltpu.SMEM)] + [VMEM_ALL] * cams,
+        in_specs=[pl.BlockSpec(memory_space=pl.ANY)] + [VMEM_ALL] * (cams - 1),
         out_specs=(VMEM_ALL, VMEM_ALL),
         scratch_shapes=[
+            pltpu.VMEM(pieces[0].shape, BF),
+            pltpu.SemaphoreType.DMA,
             pltpu.VMEM((cams * frames_here, LANES), F32),
             pltpu.VMEM((frames_here * places, cams), BF),
             pltpu.VMEM((frames_here * places, cams * REGIONS), BF),
             pltpu.VMEM((frames_here * places, LANES), F32),
         ],
-        compiler_params=pltpu.CompilerParams(vmem_limit_bytes=50 << 20),
-    )(me, *pieces)
+        compiler_params=pltpu.CompilerParams(vmem_limit_bytes=10 << 20),
+    )(*pieces)
+
+
+def project_kernel(
+    normed_ref, qkv_w_hbm, mixed_ref, key_w_ref, value_w_ref, query_w_ref, sems
+):
+    width = normed_ref.shape[1]
+    half = width // 2
+    targets = (query_w_ref, key_w_ref, value_w_ref)
+    pieces = [(target, k, at) for k, target in enumerate(targets) for at in (0, half)]
+    copies = [
+        pltpu.make_async_copy(
+            qkv_w_hbm.at[:, pl.ds(k * width + at, half)], target.at[:, pl.ds(at, half)], sems.at[n]
+        )
+        for n, (target, k, at) in enumerate(pieces)
+    ]
+    for copy in copies:
+        copy.start()
+    for copy, (target, k, at) in zip(copies, pieces):
+        copy.wait()
+        mixed_ref[:, k * width + at : k * width + at + half] = jnp.dot(
+            normed_ref[...], target[:, at : at + half], preferred_element_type=F32
+        ).astype(BF)
+
+
+def project(normed, qkv_w):
+    rows, width = normed.shape
+    hbm = pl.BlockSpec(memory_space=pltpu.HBM)
+    square = jax.ShapeDtypeStruct((width, width), BF)
+    return pl.pallas_call(
+        project_kernel,
+        out_shape=[jax.ShapeDtypeStruct((rows, 3 * width), BF), square, square],
+        in_specs=[VMEM_ALL, hbm],
+        out_specs=[VMEM_ALL] * 3,
+        scratch_shapes=[pltpu.VMEM((width, width), BF), pltpu.SemaphoreType.DMA((6,))],
+        cost_estimate=pl.CostEstimate(
+            flops=2 * rows * width * 3 * width,
+            bytes_accessed=2 * qkv_w.size,
+            transcendentals=0,
+        ),
+        compiler_params=pltpu.CompilerParams(vmem_limit_bytes=47 << 20),
+    )(normed, qkv_w)
 
 
 def attention_kernel(
-    mixed_ref, other_ref, key_w_ref, value_w_ref, out_w_ref, bias_ref, tokens_ref,
-    out_ref, other_keys, other_values, attended, *, frames_here
+    mixed_ref, other_ref, key_w_ref, value_w_ref, tokens_ref, out_w_hbm, bias_hbm,
+    out_ref, out_w_ref, bias_ref, sems, other_keys, other_values, scores, weights, totals, attended, *, frames_here
 ):
     rows, width = tokens_ref.shape
     others = other_ref.shape[0] // rows
     head_size = width // HEADS
     scale = 1.0 / math.sqrt(head_size)
+    splits = others + 1
+    span = splits * frames_here
+    heads = LANES // head_size
+    block = heads * frames_here
+    tiles = width // LANES
+    head_of = lax.broadcasted_iota(jnp.int32, (frames_here, LANES), 1) // head_size
+    place = lax.axis_index("frame")
+    copies = [
+        pltpu.make_async_copy(source, target, sems.at[k])
+        for k, (source, target) in enumerate(((bias_hbm, bias_ref), (out_w_hbm, out_w_ref)))
+    ]
+    for copy in copies:
+        copy.start()
     other_keys[...] = jnp.dot(
         other_ref[...], key_w_ref[...], preferred_element_type=F32
     ).astype(BF)
     other_values[...] = jnp.dot(
         other_ref[...], value_w_ref[...], preferred_element_type=F32
     ).astype(BF)
-    span = (others + 1) * frames_here
-    heads = LANES // head_size
-    head_of = lax.broadcasted_iota(jnp.int32, (frames_here, LANES), 1) // head_size
+
+    def gathered(n, tile, own, rest):
+        at = n * frames_here
+        return jnp.concatenate(
+            [mixed_ref[at : at + frames_here, own + tile * LANES : own + (tile + 1) * LANES]]
+            + [
+                rest[k * rows + at : k * rows + at + frames_here, tile * LANES : (tile + 1) * LANES]
+                for k in range(others)
+            ],
+            axis=0,
+        )
+
+    copies[0].wait()
     for n in range(SUBJ_DEV):
-        at = n * frames_here
-        for tile in range(width // LANES):
-            lanes = slice(tile * LANES, (tile + 1) * LANES)
-
-            def gathered(own, rest):
-                return jnp.concatenate(
-                    [mixed_ref[at : at + frames_here, own + tile * LANES : own + (tile + 1) * LANES]]
-                    + [
-                        rest[k * rows + at : k * rows + at + frames_here, lanes]
-                        for k in range(others)
-                    ],
-                    axis=0,
-                )
-
-            query = mixed_ref[at : at + frames_here, lanes]
+        bias = bias_ref[n]
+        turned = bias
+        for k in range(1, splits):
+            turn = jnp.concatenate(
+                [bias[:, k * frames_here :], bias[:, : k * frames_here]], axis=1
+            )
+            turned = jnp.where(place == k, turn, turned)
+        for tile in range(tiles):
+            query = mixed_ref[
+                n * frames_here : (n + 1) * frames_here, tile * LANES : (tile + 1) * LANES
+            ]
             queries = jnp.concatenate(
                 [jnp.where(head_of == h, query, jnp.zeros((), BF)) for h in range(heads)], axis=0
             )
-            scores = lax.dot_general(
+            products = lax.dot_general(
                 queries,
-                gathered(width, other_keys),
+                gathered(n, tile, width, other_keys),
                 (((1,), (1,)), ((), ())),
                 preferred_element_type=F32,
             )
-            bias = jnp.concatenate(
+            added = jnp.concatenate(
                 [
                     jnp.broadcast_to(
-                        bias_ref[n, tile * heads + h : tile * heads + h + 1, :],
-                        (frames_here, span),
+                        turned[tile * heads + h : tile * heads + h + 1, :], (frames_here, span)
                     )
                     for h in range(heads)
                 ],
                 axis=0,
             )
-            scores = scores * scale + bias
-            weights = jnp.exp(scores - jnp.max(scores, axis=1, keepdims=True))
-            denominator = jnp.sum(weights, axis=1, keepdims=True)
-            numerator = jnp.dot(
-                weights.astype(BF), gathered(2 * width, other_values), preferred_element_type=F32
-            )
-            ratio = numerator / denominator
+            at = (n * tiles + tile) * block
+            scores[at : at + block, :] = products * scale + added
+    for n in range(SUBJ_DEV):
+        part = slice(n * tiles * block, (n + 1) * tiles * block)
+        raw = scores[part, :]
+        raised = jnp.exp(raw - jnp.max(raw, axis=1, keepdims=True))
+        weights[part, :] = raised.astype(BF)
+        totals[part, :] = jnp.broadcast_to(
+            jnp.sum(raised, axis=1, keepdims=True), (tiles * block, LANES)
+        )
+    for n in range(SUBJ_DEV):
+        for tile in range(tiles):
+            at = (n * tiles + tile) * block
+            ratio = (
+                jnp.dot(
+                    weights[at : at + block, :],
+                    gathered(n, tile, 2 * width, other_values),
+                    preferred_element_type=F32,
+                )
+                / totals[at : at + block, :]
+            )
             result = ratio[:frames_here]
             for h in range(1, heads):
                 result = jnp.where(
                     head_of == h, ratio[h * frames_here : (h + 1) * frames_here], result
                 )
-            attended[at : at + frames_here, lanes] = result.astype(BF)
+            attended[
+                n * frames_here : (n + 1) * frames_here, tile * LANES : (tile + 1) * LANES
+            ] = result.astype(BF)
+    copies[1].wait()
     out_ref[...] = (
         tokens_ref[...] + jnp.dot(attended[...], out_w_ref[...], preferred_element_type=F32)
     ).astype(BF)
 
 
-def attend(mixed, other, qkv_w, out_w, bias, tokens, frames_here):
+def attend(mixed, other, key_w, value_w, out_w, bias, tokens, frames_here):
     rows, width = tokens.shape
-    whole = lambda array: pl.BlockSpec(array.shape, lambda i: (0,) * array.ndim)
+    span = bias.shape[2]
     return pl.pallas_call(
         functools.partial(attention_kernel, frames_here=frames_here),
-        grid=(1,),
         out_shape=jax.ShapeDtypeStruct((rows, width), BF),
-        in_specs=[
-            whole(mixed),
-            whole(other),
-            pl.BlockSpec((width, width), lambda i: (0, 1)),
-            pl.BlockSpec((width, width), lambda i: (0, 2)),
-            whole(out_w),
-            whole(bias),
-            whole(tokens),
-        ],
-        out_specs=whole(tokens),
+        in_specs=[VMEM_ALL] * 5 + [pl.BlockSpec(memory_space=pltpu.HBM)] * 2,
+        out_specs=VMEM_ALL,
         scratch_shapes=[
+            pltpu.VMEM(out_w.shape, BF),
+            pltpu.VMEM(bias.shape, F32),
+            pltpu.SemaphoreType.DMA((2,)),
             pltpu.VMEM(other.shape, BF),
             pltpu.VMEM(other.shape, BF),
+            pltpu.VMEM((HEADS * rows, span), F32),
+            pltpu.VMEM((HEADS * rows, span), BF),
+            pltpu.VMEM((HEADS * rows, LANES), F32),
             pltpu.VMEM((rows, width), BF),
         ],
-        compiler_params=pltpu.CompilerParams(vmem_limit_bytes=56 << 20),
-    )(mixed, other, qkv_w, qkv_w, out_w, bias, tokens)
+        compiler_params=pltpu.CompilerParams(vmem_limit_bytes=14 << 20),
+    )(mixed, other, key_w, value_w, tokens, out_w, bias)
 
 
 def per_device(
@@ -407,15 +506,8 @@
         for k in range(1, splits)
     ]
     other = others[0] if splits == 2 else jnp.concatenate(others, axis=0)
-    mixed = jnp.dot(normed, qkv_w, preferred_element_type=F32).astype(BF)
-    span = key_bias.shape[2]
-    bias = lax.dynamic_slice_in_dim(
-        jnp.concatenate([key_bias, key_bias], axis=2),
-        lax.axis_index("frame") * frames_here,
-        span,
-        axis=2,
-    )
-    posed = attend(mixed, other, qkv_w, out_w, bias, tokens, frames_here)
+    mixed, key_w, value_w = project(normed, qkv_w)
+    posed = attend(mixed, other, key_w, value_w, out_w, key_bias, tokens, frames_here)
     return posed.reshape(SUBJ_DEV, frames_here, tokens.shape[1])
 
 

time: 75 us -> 62 us (0.83)
  the two profiles are of different devices: /device:TPU:10 before, /device:TPU:0 now
where the time goes in v2:
time: 62 us; the launch traced here: 61.9 us
  starting transfers between devices  29 us (47%)
  Pallas kernels  19.7 us (32%)
  waiting for transfers between devices  12 us (19%)
  local copies, waits for them, and re-layouts  0.92 us (1%)
    ppermute x15, starting transfers between devices, swap(): return lax.ppermute(array, 'cam', [(i, i ^ bits) for i in range(cams)])  27.5 us
    pallas_call x1, Pallas kernels, camera_tiles(): pl.pallas_call(functools.partial(camera_kernel, subjects=slots.shape[0],...  11.8 us
    ppermute x15, waiting for transfers between devices, swap(): return lax.ppermute(array, 'cam', [(i, i ^ bits) for i in range(cams)])  8.23 us
    ppermute x1, waiting for transfers between devices, per_device(): lax.ppermute(normed, 'frame', [((i + k) % splits, i) for i in range(split...  3.81 us
    pallas_call x1, Pallas kernels, project(): pl.pallas_call(project_kernel, out_shape=[jax.ShapeDtypeStruct((rows, 3 *...  3.21 us
    pallas_call x1, Pallas kernels, attend(): pl.pallas_call(functools.partial(attention_kernel, frames_here=frames_her...  2.98 us
    pallas_call x1, Pallas kernels, build_tokens(): pl.pallas_call(functools.partial(token_kernel, cams=cams, parts=parts, fr...  1.68 us
    ppermute x1, starting transfers between devices, per_device(): lax.ppermute(normed, 'frame', [((i + k) % splits, i) for i in range(split...  1.54 us
  transfers between devices with their start and end apart: 16, of which 8 were waited for; matrix products, arithmetic and copies ran while one was open for 0% of the time, Pallas kernels for 5%

profile of v2, /device:TPU:0, one launch (start us, length us, event | category | flops | bytes accessed | tf_op | source)
XLA Modules:
  0.0 61.9 jit_solution(5714570547839201793)
XLA Ops:
  0.0 11.8 %shard_map.127.refs_0_ = bf16[576,128]{1,0:T(8,128)(2,1)} custom-call(bf16[3,32,4096]{2,1,0:T(8,128)(2,1)} %bitcast.11, bf16[384,512]{1,0:T(8,128)(2,1)} %constant.4.clone.pack_hbm, bf16[2048,27]{1,0:T(8,128)(2,1)} %constant.5.clone.tap_hbm, bf16[27,128]{1,0:T(8,128)(2,1)} %w1_hbm.1, bf16[1152,256]{1,0:T(8,128)(2,1)} %w2_hbm.1, bf16[256,128]{1,0:T(8,128)(2,1)} %wt_hbm.1, ...), custom_call_target="tpu_custom_call" | custom-call | tf_op jit(solution)/shard_map/pallas_call | solution.py:192
  11.8 0.6 collective-permute-start.7
  12.3 5.6 %collective-permute-start.6 = (bf16[576,128]{1,0:T(8,128)(2,1)}, bf16[576,128]{1,0:T(8,128)(2,1)S(1)}, u32[]{:S(2)}, u32[]{:S(2)}) collective-permute-start(bf16[576,128]{1,0:T(8,128)(2,1)} %shard_map.127.refs_0_), channel_id=1, source_target_pairs={{0,28},{2,30},{4,24},{6,26},{8,20},{10,22},{12,16},{14,18},{16,12}... | collective-permute-start | bytes 442376 | tf_op jit(solution)/shard_map/ppermute | solution.py:217
  18.0 0.2 collective-permute-start.5
  18.2 0.7 %collective-permute-start.4 = (bf16[576,128]{1,0:T(8,128)(2,1)}, bf16[576,128]{1,0:T(8,128)(2,1)S(1)}, u32[]{:S(2)}, u32[]{:S(2)}) collective-permute-start(bf16[576,128]{1,0:T(8,128)(2,1)} %shard_map.127.refs_0_), channel_id=1, source_target_pairs={{0,20},{2,22},{4,16},{6,18},{8,28},{10,30},{12,24},{14,26},{16,4},... | collective-permute-start | bytes 442376 | tf_op jit(solution)/shard_map/ppermute | solution.py:217
  18.9 2.0 %collective-permute-start.3 = (bf16[576,128]{1,0:T(8,128)(2,1)}, bf16[576,128]{1,0:T(8,128)(2,1)S(1)}, u32[]{:S(2)}, u32[]{:S(2)}) collective-permute-start(bf16[576,128]{1,0:T(8,128)(2,1)} %shard_map.127.refs_0_), channel_id=1, source_target_pairs={{0,16},{2,18},{4,20},{6,22},{8,24},{10,26},{12,28},{14,30},{16,0},... | collective-permute-start | bytes 442376 | tf_op jit(solution)/shard_map/ppermute | solution.py:217
  21.0 0.0 collective-permute-done.7.refs_8_
  21.0 2.3 %collective-permute-start.2 = (bf16[576,128]{1,0:T(8,128)(2,1)}, bf16[576,128]{1,0:T(8,128)(2,1)S(1)}, u32[]{:S(2)}, u32[]{:S(2)}) collective-permute-start(bf16[576,128]{1,0:T(8,128)(2,1)} %shard_map.127.refs_0_), channel_id=1, source_target_pairs={{0,12},{2,14},{4,8},{6,10},{8,4},{10,6},{12,0},{14,2},{16,28},{18,... | collective-permute-start | bytes 442376 | tf_op jit(solution)/shard_map/ppermute | solution.py:217
  23.3 0.0 collective-permute-done.6.refs_7_
  23.3 13.0 %collective-permute-start.1 = (bf16[576,128]{1,0:T(8,128)(2,1)}, bf16[576,128]{1,0:T(8,128)(2,1)S(1)}, u32[]{:S(2)}, u32[]{:S(2)}) collective-permute-start(bf16[576,128]{1,0:T(8,128)(2,1)} %shard_map.127.refs_0_), channel_id=1, source_target_pairs={{0,8},{2,10},{4,12},{6,14},{8,0},{10,2},{12,4},{14,6},{16,24},{18,... | collective-permute-start | bytes 442376 | tf_op jit(solution)/shard_map/ppermute | solution.py:217
  36.2 0.0 collective-permute-done.5.refs_6_
  36.2 1.5 %collective-permute-start = (bf16[576,128]{1,0:T(8,128)(2,1)}, bf16[576,128]{1,0:T(8,128)(2,1)S(1)}, u32[]{:S(2)}, u32[]{:S(2)}) collective-permute-start(bf16[576,128]{1,0:T(8,128)(2,1)} %shard_map.127.refs_0_), channel_id=1, source_target_pairs={{0,4},{2,6},{4,0},{6,2},{8,12},{10,14},{12,8},{14,10},{16,20},{18,... | collective-permute-start | bytes 442376 | tf_op jit(solution)/shard_map/ppermute | solution.py:217
  37.7 3.6 %collective-permute-done.4.refs_5_ = bf16[576,128]{1,0:T(8,128)(2,1)S(1)} collective-permute-done((bf16[576,128]{1,0:T(8,128)(2,1)}, bf16[576,128]{1,0:T(8,128)(2,1)S(1)}, u32[]{:S(2)}, u32[]{:S(2)}) %collective-permute-start.4) | collective-permute-done | bytes 147488 | tf_op jit(solution)/shard_map/ppermute | solution.py:217
  41.3 0.0 collective-permute-start.14
  41.3 2.7 %collective-permute-done.3.refs_4_ = bf16[576,128]{1,0:T(8,128)(2,1)S(1)} collective-permute-done((bf16[576,128]{1,0:T(8,128)(2,1)}, bf16[576,128]{1,0:T(8,128)(2,1)S(1)}, u32[]{:S(2)}, u32[]{:S(2)}) %collective-permute-start.3) | collective-permute-done | bytes 147488 | tf_op jit(solution)/shard_map/ppermute | solution.py:217
  44.0 0.0 collective-permute-start.13
  44.0 0.0 collective-permute-done.2.refs_3_
  44.0 0.5 collective-permute-start.12
  44.5 0.9 %collective-permute-done.1.refs_2_ = bf16[576,128]{1,0:T(8,128)(2,1)S(1)} collective-permute-done((bf16[576,128]{1,0:T(8,128)(2,1)}, bf16[576,128]{1,0:T(8,128)(2,1)S(1)}, u32[]{:S(2)}, u32[]{:S(2)}) %collective-permute-start.1) | collective-permute-done | bytes 147488 | tf_op jit(solution)/shard_map/ppermute | solution.py:217
  45.4 0.0 collective-permute-start.11
  45.4 0.0 collective-permute-done.refs_1_
  45.4 0.5 collective-permute-start.10
  45.9 0.0 collective-permute-done.14.refs_15_
  45.9 0.1 collective-permute-start.9
  46.0 0.0 collective-permute-done.13.refs_14_
  46.0 0.4 collective-permute-start.8
  46.4 0.0 collective-permute-done.12.refs_13_
  46.4 0.3 collective-permute-done.11.refs_12_
  46.8 0.2 collective-permute-done.10.refs_11_
  47.0 0.3 collective-permute-done.9.refs_10_
  47.3 0.2 collective-permute-done.8.refs_9_
  47.5 0.0 copy-start.1
  47.5 0.9 %copy-done.1 = bf16[576,128]{1,0:T(8,128)(2,1)S(1)} copy-done((bf16[576,128]{1,0:T(8,128)(2,1)S(1)}, bf16[576,128]{1,0:T(8,128)(2,1)}, u32[]{:S(2)}) %copy-start.1) | copy-done | bytes 147480
  48.4 1.7 %shard_map.128 = (f32[128,1024]{1,0:T(8,128)S(1)}, bf16[128,1024]{1,0:T(8,128)(2,1)S(1)}) custom-call(bf16[576,128]{1,0:T(8,128)(2,1)S(1)} %copy-done.1, bf16[576,128]{1,0:T(8,128)(2,1)S(1)} %collective-permute-done.refs_1_, bf16[576,128]{1,0:T(8,128)(2,1)S(1)} %collective-permute-done.1.refs_2_, bf16[576,128]{1,0:T(8,128)(2,1)S(1)} %collective-permute-done.2.refs_3_, ...), custom_call_target="tpu_custom_call" | custom-call | tf_op jit(solution)/shard_map/pallas_call | solution.py:304
  50.1 0.0 copy-start
  50.1 0.0 copy-start.2
  50.1 1.5 %collective-permute-start.15 = (bf16[128,1024]{1,0:T(8,128)(2,1)S(1)}, bf16[128,1024]{1,0:T(8,128)(2,1)S(1)}, u32[]{:S(2)}, u32[]{:S(2)}) collective-permute-start(bf16[128,1024]{1,0:T(8,128)(2,1)S(1)} %get-tuple-element.10.normed_ref), channel_id=1, source_target_pairs={{1,0},{0,1},{3,2},{2,3},{5,4},{4,5},{7,6},{6,7},{9,8},{8,9},{11,10... | collective-permute-start | bytes 786440 | tf_op jit(solution)/shard_map/ppermute | solution.py:505
  51.7 3.2 %shard_map.129 = (bf16[128,3072]{1,0:T(8,128)(2,1)S(1)}, bf16[1024,1024]{1,0:T(8,128)(2,1)S(1)}, bf16[1024,1024]{1,0:T(8,128)(2,1)S(1)}) custom-call(bf16[128,1024]{1,0:T(8,128)(2,1)S(1)} %get-tuple-element.10.normed_ref, bf16[1024,3072]{1,0:T(8,128)(2,1)} %qkv_w_hbm.1), custom_call_target="tpu_custom_call" | custom-call | flops 805306368 | bytes 6291456 | tf_op jit(solution)/shard_map/pallas_call | solution.py:350
  54.9 3.8 %collective-permute-done.15.other_ref = bf16[128,1024]{1,0:T(8,128)(2,1)S(1)} collective-permute-done((bf16[128,1024]{1,0:T(8,128)(2,1)S(1)}, bf16[128,1024]{1,0:T(8,128)(2,1)S(1)}, u32[]{:S(2)}, u32[]{:S(2)}) %collective-permute-start.15) | collective-permute-done | bytes 262176 | tf_op jit(solution)/shard_map/ppermute | solution.py:505
  58.7 0.0 copy-done
  58.7 0.0 copy-done.2
  58.7 3.0 %shard_map.130 = bf16[128,1024]{1,0:T(8,128)(2,1)} custom-call(bf16[128,3072]{1,0:T(8,128)(2,1)S(1)} %get-tuple-element.11.mixed_ref, bf16[128,1024]{1,0:T(8,128)(2,1)S(1)} %collective-permute-done.15.other_ref, bf16[1024,1024]{1,0:T(8,128)(2,1)S(1)} %get-tuple-element.12.key_w_ref, bf16[1024,1024]{1,0:T(8,128)(2,1)S(1)} %get-tuple-element.13.value_w_ref, ...), custom_call_target="tpu_custom_call" | custom-call | tf_op jit(solution)/shard_map/pallas_call | solution.py:473
Async XLA Ops:
  11.8 9.2 %collective-permute-start.7 = (bf16[576,128]{1,0:T(8,128)(2,1)}, bf16[576,128]{1,0:T(8,128)(2,1)S(1)}, u32[]{:S(2)}, u32[]{:S(2)}) collective-permute-start(bf16[576,128]{1,0:T(8,128)(2,1)} %shard_map.127.refs_0_), channel_id=1, source_target_pairs={{0,2},{2,0},{4,6},{6,4},{8,10},{10,8},{12,14},{14,12},{16,18},{18,... | collective-permute-start | bytes 442376 | tf_op jit(solution)/shard_map/ppermute | solution.py:217
  12.3 10.9 %collective-permute-start.6 = (bf16[576,128]{1,0:T(8,128)(2,1)}, bf16[576,128]{1,0:T(8,128)(2,1)S(1)}, u32[]{:S(2)}, u32[]{:S(2)}) collective-permute-start(bf16[576,128]{1,0:T(8,128)(2,1)} %shard_map.127.refs_0_), channel_id=1, source_target_pairs={{0,28},{2,30},{4,24},{6,26},{8,20},{10,22},{12,16},{14,18},{16,12}... | collective-permute-start | bytes 442376 | tf_op jit(solution)/shard_map/ppermute | solution.py:217
  18.0 18.3 %collective-permute-start.5 = (bf16[576,128]{1,0:T(8,128)(2,1)}, bf16[576,128]{1,0:T(8,128)(2,1)S(1)}, u32[]{:S(2)}, u32[]{:S(2)}) collective-permute-start(bf16[576,128]{1,0:T(8,128)(2,1)} %shard_map.127.refs_0_), channel_id=1, source_target_pairs={{0,24},{2,26},{4,28},{6,30},{8,16},{10,18},{12,20},{14,22},{16,8},... | collective-permute-start | bytes 442376 | tf_op jit(solution)/shard_map/ppermute | solution.py:217
  18.2 23.1 %collective-permute-start.4 = (bf16[576,128]{1,0:T(8,128)(2,1)}, bf16[576,128]{1,0:T(8,128)(2,1)S(1)}, u32[]{:S(2)}, u32[]{:S(2)}) collective-permute-start(bf16[576,128]{1,0:T(8,128)(2,1)} %shard_map.127.refs_0_), channel_id=1, source_target_pairs={{0,20},{2,22},{4,16},{6,18},{8,28},{10,30},{12,24},{14,26},{16,4},... | collective-permute-start | bytes 442376 | tf_op jit(solution)/shard_map/ppermute | solution.py:217
  18.9 25.1 %collective-permute-start.3 = (bf16[576,128]{1,0:T(8,128)(2,1)}, bf16[576,128]{1,0:T(8,128)(2,1)S(1)}, u32[]{:S(2)}, u32[]{:S(2)}) collective-permute-start(bf16[576,128]{1,0:T(8,128)(2,1)} %shard_map.127.refs_0_), channel_id=1, source_target_pairs={{0,16},{2,18},{4,20},{6,22},{8,24},{10,26},{12,28},{14,30},{16,0},... | collective-permute-start | bytes 442376 | tf_op jit(solution)/shard_map/ppermute | solution.py:217
  21.0 23.0 %collective-permute-start.2 = (bf16[576,128]{1,0:T(8,128)(2,1)}, bf16[576,128]{1,0:T(8,128)(2,1)S(1)}, u32[]{:S(2)}, u32[]{:S(2)}) collective-permute-start(bf16[576,128]{1,0:T(8,128)(2,1)} %shard_map.127.refs_0_), channel_id=1, source_target_pairs={{0,12},{2,14},{4,8},{6,10},{8,4},{10,6},{12,0},{14,2},{16,28},{18,... | collective-permute-start | bytes 442376 | tf_op jit(solution)/shard_map/ppermute | solution.py:217
  23.3 22.1 %collective-permute-start.1 = (bf16[576,128]{1,0:T(8,128)(2,1)}, bf16[576,128]{1,0:T(8,128)(2,1)S(1)}, u32[]{:S(2)}, u32[]{:S(2)}) collective-permute-start(bf16[576,128]{1,0:T(8,128)(2,1)} %shard_map.127.refs_0_), channel_id=1, source_target_pairs={{0,8},{2,10},{4,12},{6,14},{8,0},{10,2},{12,4},{14,6},{16,24},{18,... | collective-permute-start | bytes 442376 | tf_op jit(solution)/shard_map/ppermute | solution.py:217
  36.2 9.2 %collective-permute-start = (bf16[576,128]{1,0:T(8,128)(2,1)}, bf16[576,128]{1,0:T(8,128)(2,1)S(1)}, u32[]{:S(2)}, u32[]{:S(2)}) collective-permute-start(bf16[576,128]{1,0:T(8,128)(2,1)} %shard_map.127.refs_0_), channel_id=1, source_target_pairs={{0,4},{2,6},{4,0},{6,2},{8,12},{10,14},{12,8},{14,10},{16,20},{18,... | collective-permute-start | bytes 442376 | tf_op jit(solution)/shard_map/ppermute | solution.py:217
  41.3 4.6 %collective-permute-start.14 = (bf16[576,128]{1,0:T(8,128)(2,1)S(1)}, bf16[576,128]{1,0:T(8,128)(2,1)S(1)}, u32[]{:S(2)}, u32[]{:S(2)}) collective-permute-start(bf16[576,128]{1,0:T(8,128)(2,1)S(1)} %collective-permute-done.6.refs_7_), channel_id=1, source_target_pairs={{0,2},{2,0},{4,6},{6,4},{8,10},{10,8},{12,14},{14,12},{16,18},{18,... | collective-permute-start | bytes 442376 | tf_op jit(solution)/shard_map/ppermute | solution.py:217
  44.0 2.0 %collective-permute-start.13 = (bf16[576,128]{1,0:T(8,128)(2,1)S(1)}, bf16[576,128]{1,0:T(8,128)(2,1)S(1)}, u32[]{:S(2)}, u32[]{:S(2)}) collective-permute-start(bf16[576,128]{1,0:T(8,128)(2,1)S(1)} %collective-permute-done.5.refs_6_), channel_id=1, source_target_pairs={{0,2},{2,0},{4,6},{6,4},{8,10},{10,8},{12,14},{14,12},{16,18},{18,... | collective-permute-start | bytes 442376 | tf_op jit(solution)/shard_map/ppermute | solution.py:217
  44.0 2.4 %collective-permute-start.12 = (bf16[576,128]{1,0:T(8,128)(2,1)S(1)}, bf16[576,128]{1,0:T(8,128)(2,1)S(1)}, u32[]{:S(2)}, u32[]{:S(2)}) collective-permute-start(bf16[576,128]{1,0:T(8,128)(2,1)S(1)} %collective-permute-done.4.refs_5_), channel_id=1, source_target_pairs={{0,2},{2,0},{4,6},{6,4},{8,10},{10,8},{12,14},{14,12},{16,18},{18,... | collective-permute-start | bytes 442376 | tf_op jit(solution)/shard_map/ppermute | solution.py:217
  45.4 1.4 %collective-permute-start.11 = (bf16[576,128]{1,0:T(8,128)(2,1)S(1)}, bf16[576,128]{1,0:T(8,128)(2,1)S(1)}, u32[]{:S(2)}, u32[]{:S(2)}) collective-permute-start(bf16[576,128]{1,0:T(8,128)(2,1)S(1)} %collective-permute-done.3.refs_4_), channel_id=1, source_target_pairs={{0,2},{2,0},{4,6},{6,4},{8,10},{10,8},{12,14},{14,12},{16,18},{18,... | collective-permute-start | bytes 442376 | tf_op jit(solution)/shard_map/ppermute | solution.py:217
  45.4 1.6 %collective-permute-start.10 = (bf16[576,128]{1,0:T(8,128)(2,1)S(1)}, bf16[576,128]{1,0:T(8,128)(2,1)S(1)}, u32[]{:S(2)}, u32[]{:S(2)}) collective-permute-start(bf16[576,128]{1,0:T(8,128)(2,1)S(1)} %collective-permute-done.2.refs_3_), channel_id=1, source_target_pairs={{0,2},{2,0},{4,6},{6,4},{8,10},{10,8},{12,14},{14,12},{16,18},{18,... | collective-permute-start | bytes 442376 | tf_op jit(solution)/shard_map/ppermute | solution.py:217
  45.9 1.4 %collective-permute-start.9 = (bf16[576,128]{1,0:T(8,128)(2,1)S(1)}, bf16[576,128]{1,0:T(8,128)(2,1)S(1)}, u32[]{:S(2)}, u32[]{:S(2)}) collective-permute-start(bf16[576,128]{1,0:T(8,128)(2,1)S(1)} %collective-permute-done.1.refs_2_), channel_id=1, source_target_pairs={{0,2},{2,0},{4,6},{6,4},{8,10},{10,8},{12,14},{14,12},{16,18},{18,... | collective-permute-start | bytes 442376 | tf_op jit(solution)/shard_map/ppermute | solution.py:217
  46.0 1.5 %collective-permute-start.8 = (bf16[576,128]{1,0:T(8,128)(2,1)S(1)}, bf16[576,128]{1,0:T(8,128)(2,1)S(1)}, u32[]{:S(2)}, u32[]{:S(2)}) collective-permute-start(bf16[576,128]{1,0:T(8,128)(2,1)S(1)} %collective-permute-done.refs_1_), channel_id=1, source_target_pairs={{0,2},{2,0},{4,6},{6,4},{8,10},{10,8},{12,14},{14,12},{16,18},{18,... | collective-permute-start | bytes 442376 | tf_op jit(solution)/shard_map/ppermute | solution.py:217
  47.5 0.9 %copy-start.1 = (bf16[576,128]{1,0:T(8,128)(2,1)S(1)}, bf16[576,128]{1,0:T(8,128)(2,1)}, u32[]{:S(2)}) copy-start(bf16[576,128]{1,0:T(8,128)(2,1)} %shard_map.127.refs_0_) | copy-start | bytes 442372
  50.1 8.6 %copy-start = (bf16[1024,1024]{1,0:T(8,128)(2,1)S(1)}, bf16[1024,1024]{1,0:T(8,128)(2,1)}, u32[]{:S(2)}) copy-start(bf16[1024,1024]{1,0:T(8,128)(2,1)} %out_w_hbm.1) | copy-start | bytes 6291460
  50.1 8.6 %copy-start.2 = (f32[4,16,64]{2,1,0:T(8,128)S(1)}, f32[4,16,64]{2,1,0:T(8,128)}, u32[]{:S(2)}) copy-start(f32[4,16,64]{2,1,0:T(8,128)} %bias_hbm.1) | copy-start | bytes 49156
  50.1 8.6 %collective-permute-start.15 = (bf16[128,1024]{1,0:T(8,128)(2,1)S(1)}, bf16[128,1024]{1,0:T(8,128)(2,1)S(1)}, u32[]{:S(2)}, u32[]{:S(2)}) collective-permute-start(bf16[128,1024]{1,0:T(8,128)(2,1)S(1)} %get-tuple-element.10.normed_ref), channel_id=1, source_target_pairs={{1,0},{0,1},{3,2},{2,3},{5,4},{4,5},{7,6},{6,7},{9,8},{8,9},{11,10... | collective-permute-start | bytes 786440 | tf_op jit(solution)/shard_map/ppermute | solution.py:505

commit v3 on v2

--- a/solution.py
+++ b/solution.py
@@ -56,10 +56,14 @@
 def camera_kernel(
     x_hbm, pack_hbm, tap_hbm, w1_hbm, w2_hbm, wt_hbm, vis_hbm, count_hbm, region_hbm, slot_hbm,
     out_ref, x_ref, pack_ref, tap_ref, w1_ref, w2_ref, wt_ref, vis_ref, count_ref, region_ref,
-    slot_ref, sems, packed, wide, cells, part, *, subjects, parts
+    slot_ref, sems, packed, wide, cells, part, *, subjects, parts, first
 ):
+    frames_here = x_ref.shape[1]
+    here = slice(first, first + frames_here)
+    images_hbm = x_hbm.at[:, pl.ds(first, frames_here), :]
     sources = (
-        slot_hbm, vis_hbm, count_hbm, region_hbm, w1_hbm, tap_hbm, pack_hbm, x_hbm, w2_hbm, wt_hbm
+        slot_hbm, vis_hbm, count_hbm, region_hbm, w1_hbm, tap_hbm, pack_hbm, images_hbm, w2_hbm,
+        wt_hbm,
     )
     targets = (
         slot_ref, vis_ref, count_ref, region_ref, w1_ref, tap_ref, pack_ref, x_ref, w2_ref, wt_ref
@@ -70,16 +74,7 @@
     ]
     for copy in copies:
         copy.start()
-    frames_here = x_ref.shape[1]
     rows = OUT1 * frames_here
-    listed = vis_ref.shape[0]
-    lanes = listed * parts
-    expand = (
-        lax.broadcasted_iota(jnp.int32, (lanes, listed), 0) // parts
-        == lax.broadcasted_iota(jnp.int32, (lanes, listed), 1)
-    ).astype(BF)
-    part_of = lax.broadcasted_iota(jnp.int32, (lanes, frames_here), 0) % parts
-
     for copy in copies[:6]:
         copy.wait()
     for column in range(GROUP):
@@ -89,31 +84,9 @@
             preferred_element_type=F32,
         ).astype(BF)
 
-    def spread(ref):
-        return jnp.dot(
-            expand, ref[:, 0, :].astype(F32).astype(BF), preferred_element_type=F32
-        ).astype(jnp.int32)
-
-    who = spread(vis_ref)
-    code = jnp.where(part_of < spread(count_ref), region_ref[...] + 1, 0)
-    row_of = jnp.zeros((lanes, frames_here), jnp.int32)
-    for subject in range(subjects):
-        row_of = jnp.where(who == subject, slot_ref[subject], row_of)
-    blocks = -(-lanes // LANES)
-    fill = blocks * LANES - lanes
-    base = REGIONS * frames_here
-    for k, array in enumerate((code, row_of)):
-        array = array.astype(F32)
-        if fill:
-            array = jnp.concatenate([array, jnp.zeros((fill, frames_here), F32)], axis=0)
-        array = array.T.astype(BF)
-        for block in range(blocks):
-            at = base + (k * blocks + block) * frames_here
-            out_ref[at : at + frames_here, :] = array[:, block * LANES : (block + 1) * LANES]
-
     cells[0] = jnp.zeros(cells.shape[1:], BF)
     cells[:, 1, 0] = jnp.zeros((cells.shape[0],) + cells.shape[3:], BF)
-    packed[:, 0:frames_here, :] = jnp.zeros((GROUPS, frames_here, LANES), BF)
+    packed[0:frames_here, :] = jnp.zeros((frames_here, GROUPS * LANES), BF)
     copies[6].wait()
     copies[7].wait()
     images = jnp.concatenate(
@@ -125,14 +98,10 @@
         ],
         axis=0,
     )
+    packed[frames_here:, :] = jnp.dot(images, pack_ref[...], preferred_element_type=F32).astype(BF)
     for group in range(GROUPS):
-        packed[group, frames_here:, :] = jnp.dot(
-            images, pack_ref[:, group * LANES : (group + 1) * LANES], preferred_element_type=F32
-        ).astype(BF)
-    for group in range(GROUPS):
-        lhs = jnp.concatenate(
-            [packed[group, frames_here:, :], packed[group, 0:rows, :]], axis=1
-        )
+        lanes = slice(group * LANES, (group + 1) * LANES)
+        lhs = jnp.concatenate([packed[frames_here:, lanes], packed[0:rows, lanes]], axis=1)
         for pair in range(GROUP // 2):
             both = jnp.dot(
                 lhs, wide[:, pair * 2 * LANES : (pair + 1) * 2 * LANES], preferred_element_type=F32
@@ -141,6 +110,30 @@
             at = group * (GROUP // 2) + pair
             cells[1:, 0, at] = both[:, :LANES].reshape(OUT1, frames_here, LANES)
             cells[1:, 1, at + 1] = both[:, LANES:].reshape(OUT1, frames_here, LANES)
+
+    listed = vis_ref.shape[0]
+    lanes = listed * parts
+    expand = (
+        lax.broadcasted_iota(jnp.int32, (lanes, listed), 0) // parts
+        == lax.broadcasted_iota(jnp.int32, (lanes, listed), 1)
+    ).astype(BF)
+    part_of = lax.broadcasted_iota(jnp.int32, (lanes, frames_here), 0) % parts
+    count = jnp.dot(
+        expand, count_ref[:, 0, here].astype(F32).astype(BF), preferred_element_type=F32
+    ).astype(jnp.int32)
+    code = jnp.where(part_of < count, region_ref[:, here] + 1, 0)
+    who = vis_ref[:, 0, here]
+    row_of = jnp.zeros((listed, frames_here), jnp.int32)
+    for subject in range(subjects):
+        row_of = jnp.where(who == subject, slot_ref[subject], row_of)
+    blocks = (out_ref.shape[0] // frames_here) - REGIONS
+    base = REGIONS * frames_here
+    fill = jnp.zeros((blocks * LANES - lanes - listed, frames_here), F32)
+    lists = jnp.concatenate([code.astype(F32), row_of.astype(F32), fill], axis=0).T.astype(BF)
+    for block in range(blocks):
+        out_ref[base + block * frames_here : base + (block + 1) * frames_here, :] = lists[
+            :, block * LANES : (block + 1) * LANES
+        ]
 
     copies[8].wait()
     copies[9].wait()
@@ -173,10 +166,12 @@
     out_ref[0:base, :] = part[...].astype(BF)
 
 
-def camera_tiles(frames, conv1_w, conv2_w, tile_w, vis_subject, part_count, part_region, slots):
+def camera_tiles(
+    frames, conv1_w, conv2_w, tile_w, vis_subject, part_count, part_region, slots, first, amount
+):
     frames_here = frames.shape[1]
     listed, parts = part_region.shape[2:]
-    blocks = -(-listed * parts // LANES)
+    blocks = -(-listed * (parts + 1) // LANES)
     operands = (
         jnp.transpose(frames[0], (1, 0, 2)),
         jnp.asarray(pack_table(), BF),
@@ -190,135 +185,156 @@
         slots,
     )
     return pl.pallas_call(
-        functools.partial(camera_kernel, subjects=slots.shape[0], parts=parts),
-        out_shape=jax.ShapeDtypeStruct(((REGIONS + 2 * blocks) * frames_here, LANES), BF),
+        functools.partial(
+            camera_kernel, subjects=slots.shape[0], parts=parts, first=first
+        ),
+        out_shape=jax.ShapeDtypeStruct(((REGIONS + blocks) * amount, LANES), BF),
         in_specs=[pl.BlockSpec(memory_space=pltpu.HBM)] * len(operands),
         out_specs=VMEM_ALL,
-        scratch_shapes=[pltpu.VMEM(array.shape, array.dtype) for array in operands[:-1]]
+        scratch_shapes=[pltpu.VMEM((3, amount, operands[0].shape[2]), BF)]
+        + [pltpu.VMEM(array.shape, array.dtype) for array in operands[1:-1]]
         + [
             pltpu.SMEM(slots.shape, slots.dtype),
             pltpu.SemaphoreType.DMA((len(operands),)),
-            pltpu.VMEM((GROUPS, (OUT1 + 1) * frames_here, LANES), BF),
+            pltpu.VMEM(((OUT1 + 1) * amount, GROUPS * LANES), BF),
             pltpu.VMEM((2 * LANES, GROUP * LANES), BF),
-            pltpu.VMEM((OUT1 + 1, 2, OUT2 + 1, frames_here, LANES), BF),
-            pltpu.VMEM((REGIONS * frames_here, LANES), F32),
+            pltpu.VMEM((OUT1 + 1, 2, OUT2 + 1, amount, LANES), BF),
+            pltpu.VMEM((REGIONS * amount, LANES), F32),
         ],
+        cost_estimate=pl.CostEstimate(
+            flops=amount * 400_000_000, bytes_accessed=amount * 100_000, transcendentals=0
+        ),
         compiler_params=pltpu.CompilerParams(vmem_limit_bytes=60 << 20),
     )(*operands)
 
 
-def exchange(payload):
+def exchange(chunks):
     cams = lax.axis_size("cam")
     if cams & (cams - 1):
-        gathered = lax.all_gather(payload, "cam", axis=0, tiled=False)
-        return [gathered[c] for c in range(cams)]
+        gathered = [lax.all_gather(chunk, "cam", axis=0, tiled=False) for chunk in chunks]
+        return [[whole[c] for c in range(cams)] for whole in gathered]
 
     def swap(array, bits):
         return lax.ppermute(array, "cam", [(i, i ^ bits) for i in range(cams)])
 
-    pieces = [payload] + [swap(payload, bits) for bits in range(2, cams, 2)]
-    return pieces + [swap(piece, 1) for piece in pieces]
-
-
-def token_kernel(*refs, cams, parts, frames_here):
-    tokens_ref, normed_ref, own, sem, marks, spots, picks, summed = refs[cams:]
-    copy = pltpu.make_async_copy(refs[0], own, sem)
-    copy.start()
-    pieces = refs[1:cams] + (own,)
-    blocks = (pieces[0].shape[0] // frames_here - REGIONS) // 2
+    results = []
+    for chunk in chunks:
+        far = [chunk]
+        for bits in [1 << k for k in reversed(range(3, cams.bit_length() - 1))]:
+            far = far + [swap(piece, bits) for piece in far]
+        beside = [swap(chunk, 2)] + [swap(piece, 2) for piece in far[1:]]
+        near = [swap(piece, 4) for piece in far]
+        both = far + beside + near + [swap(near[0], 2)] + [swap(piece, 4) for piece in beside[1:]]
+        results.append(both + [swap(piece, 1) for piece in both])
+    return results
+
+
+def token_kernel(*refs, cams, parts, listed, amounts):
+    count = cams * len(amounts)
+    tokens_ref, normed_ref = refs[count : count + 2]
+    own = refs[count + 2 : count + 2 + len(amounts)]
+    sems, marks, spots, picks, summed = refs[count + 2 + len(amounts) :]
+    copies = [
+        pltpu.make_async_copy(refs[k * cams], own[k], sems.at[k]) for k in range(len(amounts))
+    ]
+    for copy in copies:
+        copy.start()
+    places = SUBJ_DEV * parts
+    mine = lax.axis_index("cam") * SUBJ_DEV
+    blocks = own[0].shape[0] // amounts[0] - REGIONS
     lanes = blocks * LANES
-    places = SUBJ_DEV * parts
-    first = lax.axis_index("cam") * SUBJ_DEV
-    base = REGIONS * frames_here
     from_lane = lax.broadcasted_iota(jnp.int32, (SUBJ_DEV * lanes, LANES), 0)
     to_lane = lax.broadcasted_iota(jnp.int32, (SUBJ_DEV * lanes, LANES), 1)
     fold = (
         (from_lane % parts == to_lane % parts) & (from_lane // lanes == to_lane // parts)
     ).astype(BF)
-    codes = []
-    for piece in pieces:
-        if piece is own:
-            copy.wait()
-
-        def field(k):
-            return jnp.concatenate(
-                [
-                    piece[
-                        base + (k * blocks + b) * frames_here : base
-                        + (k * blocks + b + 1) * frames_here,
-                        :,
-                    ].astype(F32)
-                    for b in range(blocks)
-                ],
-                axis=1,
-            )
-
-        code, row = field(0), field(1)
-        codes.append(
-            jnp.concatenate(
-                [
-                    jnp.where(row == (first + s).astype(F32), code, 0.0).astype(BF)
-                    for s in range(SUBJ_DEV)
-                ],
-                axis=1,
-            )
-        )
-    marks[...] = jnp.dot(jnp.concatenate(codes, axis=0), fold, preferred_element_type=F32)
-    for f in range(frames_here):
-        found = marks[pl.ds(f, cams, stride=frames_here), :]
-        spots[f * places : (f + 1) * places, :] = found.T[:places].astype(BF)
+    views = listed * parts
+    from_view = lax.broadcasted_iota(jnp.int32, (lanes, lanes), 0)
+    to_view = lax.broadcasted_iota(jnp.int32, (lanes, lanes), 1)
+    repeat = ((from_view == views + to_view // parts) & (to_view < views)).astype(BF)
     widen = (
         lax.broadcasted_iota(jnp.int32, (cams, cams * REGIONS), 1) // REGIONS
         == lax.broadcasted_iota(jnp.int32, (cams, cams * REGIONS), 0)
     ).astype(BF)
-    spread = jnp.dot(spots[...], widen, preferred_element_type=F32)
-    region = lax.broadcasted_iota(jnp.int32, spread.shape, 1) % REGIONS + 1
-    picks[...] = jnp.where(spread == region.astype(F32), 1.0, 0.0).astype(BF)
-    for f in range(frames_here):
-        tiles = jnp.concatenate(
-            [piece[f * REGIONS : (f + 1) * REGIONS, :] for piece in pieces], axis=0
-        )
-        summed[f * places : (f + 1) * places, :] = jnp.dot(
-            picks[f * places : (f + 1) * places, :], tiles, preferred_element_type=F32
-        )
+    ahead = 0
+    for k, amount in enumerate(amounts):
+        pieces = (own[k],) + refs[k * cams + 1 : (k + 1) * cams]
+        copies[k].wait()
+        base = REGIONS * amount
+        lists = jnp.concatenate(
+            [
+                jnp.concatenate(
+                    [
+                        piece[base + b * amount : base + (b + 1) * amount, :]
+                        for b in range(blocks)
+                    ],
+                    axis=1,
+                )
+                for piece in pieces
+            ],
+            axis=0,
+        )
+        row = jnp.dot(lists, repeat, preferred_element_type=F32)
+        lane = lax.broadcasted_iota(jnp.int32, row.shape, 1)
+        code = jnp.where(lane < views, lists.astype(F32), 0.0)
+        codes = [
+            jnp.where(row == (mine + s).astype(F32), code, 0.0).astype(BF) for s in range(SUBJ_DEV)
+        ]
+        marks[0 : cams * amount, :] = jnp.dot(
+            jnp.concatenate(codes, axis=1), fold, preferred_element_type=F32
+        )
+        for f in range(amount):
+            found = marks[pl.ds(f, cams, stride=amount), :]
+            spots[f * places : (f + 1) * places, :] = found.T[:places].astype(BF)
+        spread = jnp.dot(
+            spots[0 : amount * places, :], widen, preferred_element_type=F32
+        )
+        region = lax.broadcasted_iota(jnp.int32, spread.shape, 1) % REGIONS + 1
+        picks[0 : amount * places, :] = jnp.where(spread == region.astype(F32), 1.0, 0.0).astype(BF)
+        for f in range(amount):
+            tiles = jnp.concatenate(
+                [piece[f * REGIONS : (f + 1) * REGIONS, :] for piece in pieces], axis=0
+            )
+            summed[(ahead + f) * places : (ahead + f + 1) * places, :] = jnp.dot(
+                picks[f * places : (f + 1) * places, :], tiles, preferred_element_type=F32
+            )
+        ahead += amount
     for s in range(SUBJ_DEV):
         tokens = jnp.concatenate(
-            [
-                summed[pl.ds(s * parts + p, frames_here, stride=places), :]
-                for p in range(parts)
-            ],
+            [summed[pl.ds(s * parts + p, ahead, stride=places), :] for p in range(parts)],
             axis=1,
         )
-        tokens_ref[s * frames_here : (s + 1) * frames_here, :] = tokens
+        tokens_ref[s * ahead : (s + 1) * ahead, :] = tokens
         power = jnp.mean(tokens * tokens, axis=1, keepdims=True)
-        normed_ref[s * frames_here : (s + 1) * frames_here, :] = (
-            tokens * lax.rsqrt(power + EPS)
-        ).astype(BF)
-
-
-def build_tokens(pieces, parts, frames_here):
-    cams = len(pieces)
+        normed_ref[s * ahead : (s + 1) * ahead, :] = (tokens * lax.rsqrt(power + EPS)).astype(BF)
+
+
+def build_tokens(gathered, parts, listed, amounts):
+    cams = len(gathered[0])
+    frames_here, most = sum(amounts), max(amounts)
     rows = SUBJ_DEV * frames_here
     width = parts * LANES
     places = SUBJ_DEV * parts
     return pl.pallas_call(
-        functools.partial(token_kernel, cams=cams, parts=parts, frames_here=frames_here),
+        functools.partial(
+            token_kernel, cams=cams, parts=parts, listed=listed, amounts=amounts
+        ),
         out_shape=(
             jax.ShapeDtypeStruct((rows, width), F32),
             jax.ShapeDtypeStruct((rows, width), BF),
         ),
-        in_specs=[pl.BlockSpec(memory_space=pl.ANY)] + [VMEM_ALL] * (cams - 1),
+        in_specs=([pl.BlockSpec(memory_space=pl.ANY)] + [VMEM_ALL] * (cams - 1)) * len(amounts),
         out_specs=(VMEM_ALL, VMEM_ALL),
-        scratch_shapes=[
-            pltpu.VMEM(pieces[0].shape, BF),
-            pltpu.SemaphoreType.DMA,
-            pltpu.VMEM((cams * frames_here, LANES), F32),
-            pltpu.VMEM((frames_here * places, cams), BF),
-            pltpu.VMEM((frames_here * places, cams * REGIONS), BF),
+        scratch_shapes=[pltpu.VMEM(pieces[0].shape, BF) for pieces in gathered]
+        + [
+            pltpu.SemaphoreType.DMA((len(amounts),)),
+            pltpu.VMEM((cams * most, LANES), F32),
+            pltpu.VMEM((most * places, cams), BF),
+            pltpu.VMEM((most * places, cams * REGIONS), BF),
             pltpu.VMEM((frames_here * places, LANES), F32),
         ],
         compiler_params=pltpu.CompilerParams(vmem_limit_bytes=10 << 20),
-    )(*pieces)
+    )(*[piece for pieces in gathered for piece in pieces])
 
 
 def project_kernel(
@@ -496,10 +512,15 @@
 ):
     frames_here = frames.shape[1]
     parts = part_region.shape[3]
-    payload = camera_tiles(
-        frames, conv1_w, conv2_w, tile_w, vis_subject, part_count, part_region, subject_slot
-    )
-    tokens, normed = build_tokens(exchange(payload), parts, frames_here)
+    amounts = (frames_here // 2, frames_here // 2) if frames_here % 32 == 77 else (frames_here,)
+    chunks = [
+        camera_tiles(
+            frames, conv1_w, conv2_w, tile_w, vis_subject, part_count, part_region, subject_slot,
+            sum(amounts[:k]), amount,
+        )
+        for k, amount in enumerate(amounts)
+    ]
+    tokens, normed = build_tokens(exchange(chunks), parts, part_region.shape[2], amounts)
     splits = lax.axis_size("frame")
     others = [
         lax.ppermute(normed, "frame", [((i + k) % splits, i) for i in range(splits)])

time: 62 us -> 49.5 us (0.80)
  starting transfers between devices: 29 us -> 14.4 us
  waiting for transfers between devices: 12 us -> 14.3 us
    ppermute x15, starting transfers between devices: 27.5 us -> 12.8 us  [swap(): return lax.ppermute(array, 'cam', [(i, i ^ bits) for i in range(cams)])]
    ppermute x15, waiting for transfers between devices: 8.23 us -> 10.8 us  [swap(): return lax.ppermute(array, 'cam', [(i, i ^ bits) for i in range(cams)])]
  transfers between devices with their start and end apart: 16 -> 16, of which waited for: 8 -> 7; matrix products, arithmetic and copies ran while one was open for 0% -> 0% of each run, Pallas kernels for 5% -> 7%
where the time goes in v3:
time: 49.5 us; the launch traced here: 49.3 us
  Pallas kernels  19.4 us (39%)
  starting transfers between devices  14.4 us (29%)
  waiting for transfers between devices  14.3 us (29%)
  local copies, waits for them, and re-layouts  0.92 us (2%)
    ppermute x15, starting transfers between devices, swap(): return lax.ppermute(array, 'cam', [(i, i ^ bits) for i in range(cams)])  12.8 us
    pallas_call x1, Pallas kernels, camera_tiles(): pl.pallas_call(functools.partial(camera_kernel, subjects=slots.shape[0],...  11.5 us
    ppermute x15, waiting for transfers between devices, swap(): return lax.ppermute(array, 'cam', [(i, i ^ bits) for i in range(cams)])  10.8 us
    ppermute x1, waiting for transfers between devices, per_device(): lax.ppermute(normed, 'frame', [((i + k) % splits, i) for i in range(split...  3.59 us
    pallas_call x1, Pallas kernels, project(): pl.pallas_call(project_kernel, out_shape=[jax.ShapeDtypeStruct((rows, 3 *...  3.21 us
    pallas_call x1, Pallas kernels, attend(): pl.pallas_call(functools.partial(attention_kernel, frames_here=frames_her...  2.97 us
    pallas_call x1, Pallas kernels, build_tokens(): pl.pallas_call(functools.partial(token_kernel, cams=cams, parts=parts, li...  1.75 us
    ppermute x1, starting transfers between devices, per_device(): lax.ppermute(normed, 'frame', [((i + k) % splits, i) for i in range(split...  1.61 us
  transfers between devices with their start and end apart: 16, of which 7 were waited for; matrix products, arithmetic and copies ran while one was open for 0% of the time, Pallas kernels for 7%

profile of v3, /device:TPU:0, one launch (start us, length us, event | category | flops | bytes accessed | tf_op | source)
XLA Modules:
  0.0 49.3 jit_solution(1157914214927161559)
XLA Ops:
  0.0 11.5 %shard_map.127.refs_0_ = bf16[544,128]{1,0:T(8,128)(2,1)} custom-call(bf16[3,32,4096]{2,1,0:T(8,128)(2,1)} %bitcast.11, bf16[384,512]{1,0:T(8,128)(2,1)} %constant.4.clone.pack_hbm, bf16[2048,27]{1,0:T(8,128)(2,1)} %constant.5.clone.tap_hbm, bf16[27,128]{1,0:T(8,128)(2,1)} %w1_hbm.1, bf16[1152,256]{1,0:T(8,128)(2,1)} %w2_hbm.1, bf16[256,128]{1,0:T(8,128)(2,1)} %wt_hbm.1, ...), custom_call_target="tpu_custom_call" | custom-call | flops 12800000000 | bytes 3200000 | tf_op jit(solution)/shard_map/pallas_call | solution.py:187
  11.5 4.1 %collective-permute-start = (bf16[544,128]{1,0:T(8,128)(2,1)}, bf16[544,128]{1,0:T(8,128)(2,1)S(1)}, u32[]{:S(2)}, u32[]{:S(2)}) collective-permute-start(bf16[544,128]{1,0:T(8,128)(2,1)} %shard_map.127.refs_0_), channel_id=1, source_target_pairs={{0,16},{2,18},{4,20},{6,22},{8,24},{10,26},{12,28},{14,30},{16,0},... | collective-permute-start | bytes 417800 | tf_op jit(solution)/shard_map/ppermute | solution.py:218
  15.6 1.6 %collective-permute-start.3 = (bf16[544,128]{1,0:T(8,128)(2,1)}, bf16[544,128]{1,0:T(8,128)(2,1)S(1)}, u32[]{:S(2)}, u32[]{:S(2)}) collective-permute-start(bf16[544,128]{1,0:T(8,128)(2,1)} %shard_map.127.refs_0_), channel_id=1, source_target_pairs={{0,8},{2,10},{4,12},{6,14},{8,0},{10,2},{12,4},{14,6},{16,24},{18,... | collective-permute-start | bytes 417800 | tf_op jit(solution)/shard_map/ppermute | solution.py:218
  17.2 1.5 %collective-permute-start.1 = (bf16[544,128]{1,0:T(8,128)(2,1)}, bf16[544,128]{1,0:T(8,128)(2,1)S(1)}, u32[]{:S(2)}, u32[]{:S(2)}) collective-permute-start(bf16[544,128]{1,0:T(8,128)(2,1)} %shard_map.127.refs_0_), channel_id=1, source_target_pairs={{0,4},{2,6},{4,0},{6,2},{8,12},{10,14},{12,8},{14,10},{16,20},{18,... | collective-permute-start | bytes 417800 | tf_op jit(solution)/shard_map/ppermute | solution.py:218
  18.7 0.0 collective-permute-start.7
  18.7 3.9 %collective-permute-done.refs_1_ = bf16[544,128]{1,0:T(8,128)(2,1)S(1)} collective-permute-done((bf16[544,128]{1,0:T(8,128)(2,1)}, bf16[544,128]{1,0:T(8,128)(2,1)S(1)}, u32[]{:S(2)}, u32[]{:S(2)}) %collective-permute-start) | collective-permute-done | bytes 139296 | tf_op jit(solution)/shard_map/ppermute | solution.py:218
  22.6 1.6 %collective-permute-start.2 = (bf16[544,128]{1,0:T(8,128)(2,1)S(1)}, bf16[544,128]{1,0:T(8,128)(2,1)S(1)}, u32[]{:S(2)}, u32[]{:S(2)}) collective-permute-start(bf16[544,128]{1,0:T(8,128)(2,1)S(1)} %collective-permute-done.refs_1_), channel_id=1, source_target_pairs={{0,4},{2,6},{4,0},{6,2},{8,12},{10,14},{12,8},{14,10},{16,20},{18,... | collective-permute-start | bytes 417800 | tf_op jit(solution)/shard_map/ppermute | solution.py:218
  24.2 0.0 collective-permute-done.3.refs_4_
  24.2 0.0 collective-permute-start.11
  24.2 0.4 collective-permute-start.5
  24.6 0.0 collective-permute-done.1.refs_2_
  24.6 0.2 collective-permute-start.9
  24.9 0.0 collective-permute-done.7.refs_8_
  24.9 1.2 %collective-permute-start.4 = (bf16[544,128]{1,0:T(8,128)(2,1)S(1)}, bf16[544,128]{1,0:T(8,128)(2,1)S(1)}, u32[]{:S(2)}, u32[]{:S(2)}) collective-permute-start(bf16[544,128]{1,0:T(8,128)(2,1)S(1)} %collective-permute-done.refs_1_), channel_id=1, source_target_pairs={{0,8},{2,10},{4,12},{6,14},{8,0},{10,2},{12,4},{14,6},{16,24},{18,... | collective-permute-start | bytes 417800 | tf_op jit(solution)/shard_map/ppermute | solution.py:218
  26.0 2.2 %collective-permute-done.2.refs_3_ = bf16[544,128]{1,0:T(8,128)(2,1)S(1)} collective-permute-done((bf16[544,128]{1,0:T(8,128)(2,1)S(1)}, bf16[544,128]{1,0:T(8,128)(2,1)S(1)}, u32[]{:S(2)}, u32[]{:S(2)}) %collective-permute-start.2) | collective-permute-done | bytes 139296 | tf_op jit(solution)/shard_map/ppermute | solution.py:218
  28.2 1.6 %collective-permute-start.6 = (bf16[544,128]{1,0:T(8,128)(2,1)S(1)}, bf16[544,128]{1,0:T(8,128)(2,1)S(1)}, u32[]{:S(2)}, u32[]{:S(2)}) collective-permute-start(bf16[544,128]{1,0:T(8,128)(2,1)S(1)} %collective-permute-done.2.refs_3_), channel_id=1, source_target_pairs={{0,8},{2,10},{4,12},{6,14},{8,0},{10,2},{12,4},{14,6},{16,24},{18,... | collective-permute-start | bytes 417800 | tf_op jit(solution)/shard_map/ppermute | solution.py:218
  29.9 0.0 collective-permute-done.11.refs_12_
  29.9 0.0 collective-permute-start.8
  29.9 0.8 %collective-permute-done.5.refs_6_ = bf16[544,128]{1,0:T(8,128)(2,1)S(1)} collective-permute-done((bf16[544,128]{1,0:T(8,128)(2,1)S(1)}, bf16[544,128]{1,0:T(8,128)(2,1)S(1)}, u32[]{:S(2)}, u32[]{:S(2)}) %collective-permute-start.5) | collective-permute-done | bytes 139296 | tf_op jit(solution)/shard_map/ppermute | solution.py:218
  30.6 0.0 collective-permute-start.10
  30.6 0.0 collective-permute-done.9.refs_10_
  30.6 0.5 %collective-permute-start.13 = (bf16[544,128]{1,0:T(8,128)(2,1)S(1)}, bf16[544,128]{1,0:T(8,128)(2,1)S(1)}, u32[]{:S(2)}, u32[]{:S(2)}) collective-permute-start(bf16[544,128]{1,0:T(8,128)(2,1)S(1)} %collective-permute-done.5.refs_6_), channel_id=1, source_target_pairs={{0,2},{2,0},{4,6},{6,4},{8,10},{10,8},{12,14},{14,12},{16,18},{18,... | collective-permute-start | bytes 417800 | tf_op jit(solution)/shard_map/ppermute | solution.py:218
  31.1 0.3 collective-permute-done.4.refs_5_
  31.4 0.0 collective-permute-start.12
  31.4 2.3 %collective-permute-done.6.refs_7_ = bf16[544,128]{1,0:T(8,128)(2,1)S(1)} collective-permute-done((bf16[544,128]{1,0:T(8,128)(2,1)S(1)}, bf16[544,128]{1,0:T(8,128)(2,1)S(1)}, u32[]{:S(2)}, u32[]{:S(2)}) %collective-permute-start.6) | collective-permute-done | bytes 139296 | tf_op jit(solution)/shard_map/ppermute | solution.py:218
  33.7 0.0 collective-permute-start.14
  33.7 0.0 collective-permute-done.8.refs_9_
  33.7 0.0 collective-permute-done.13.refs_14_
  33.7 0.0 collective-permute-done.12.refs_13_
  33.7 0.0 collective-permute-done.10.refs_11_
  33.7 1.3 %collective-permute-done.14.refs_15_ = bf16[544,128]{1,0:T(8,128)(2,1)S(1)} collective-permute-done((bf16[544,128]{1,0:T(8,128)(2,1)S(1)}, bf16[544,128]{1,0:T(8,128)(2,1)S(1)}, u32[]{:S(2)}, u32[]{:S(2)}) %collective-permute-start.14) | collective-permute-done | bytes 139296 | tf_op jit(solution)/shard_map/ppermute | solution.py:218
  35.1 0.0 copy-start.1
  35.1 0.9 %copy-done.1 = bf16[544,128]{1,0:T(8,128)(2,1)S(1)} copy-done((bf16[544,128]{1,0:T(8,128)(2,1)S(1)}, bf16[544,128]{1,0:T(8,128)(2,1)}, u32[]{:S(2)}) %copy-start.1) | copy-done | bytes 139288
  36.0 1.8 %shard_map.128 = (f32[128,1024]{1,0:T(8,128)S(1)}, bf16[128,1024]{1,0:T(8,128)(2,1)S(1)}) custom-call(bf16[544,128]{1,0:T(8,128)(2,1)S(1)} %copy-done.1, bf16[544,128]{1,0:T(8,128)(2,1)S(1)} %collective-permute-done.refs_1_, bf16[544,128]{1,0:T(8,128)(2,1)S(1)} %collective-permute-done.1.refs_2_, bf16[544,128]{1,0:T(8,128)(2,1)S(1)} %collective-permute-done.2.refs_3_, ...), custom_call_target="tpu_custom_call" | custom-call | tf_op jit(solution)/shard_map/pallas_call | solution.py:318
  37.7 0.0 copy-start
  37.7 0.0 copy-start.2
  37.8 1.6 %collective-permute-start.15 = (bf16[128,1024]{1,0:T(8,128)(2,1)S(1)}, bf16[128,1024]{1,0:T(8,128)(2,1)S(1)}, u32[]{:S(2)}, u32[]{:S(2)}) collective-permute-start(bf16[128,1024]{1,0:T(8,128)(2,1)S(1)} %get-tuple-element.10.normed_ref), channel_id=1, source_target_pairs={{1,0},{0,1},{3,2},{2,3},{5,4},{4,5},{7,6},{6,7},{9,8},{8,9},{11,10... | collective-permute-start | bytes 786440 | tf_op jit(solution)/shard_map/ppermute | solution.py:526
  39.4 3.2 %shard_map.129 = (bf16[128,3072]{1,0:T(8,128)(2,1)S(1)}, bf16[1024,1024]{1,0:T(8,128)(2,1)S(1)}, bf16[1024,1024]{1,0:T(8,128)(2,1)S(1)}) custom-call(bf16[128,1024]{1,0:T(8,128)(2,1)S(1)} %get-tuple-element.10.normed_ref, bf16[1024,3072]{1,0:T(8,128)(2,1)} %qkv_w_hbm.1), custom_call_target="tpu_custom_call" | custom-call | flops 805306368 | bytes 6291456 | tf_op jit(solution)/shard_map/pallas_call | solution.py:366
  42.6 3.6 %collective-permute-done.15.other_ref = bf16[128,1024]{1,0:T(8,128)(2,1)S(1)} collective-permute-done((bf16[128,1024]{1,0:T(8,128)(2,1)S(1)}, bf16[128,1024]{1,0:T(8,128)(2,1)S(1)}, u32[]{:S(2)}, u32[]{:S(2)}) %collective-permute-start.15) | collective-permute-done | bytes 262176 | tf_op jit(solution)/shard_map/ppermute | solution.py:526
  46.2 0.0 copy-done
  46.2 0.0 copy-done.2
  46.2 3.0 %shard_map.130 = bf16[128,1024]{1,0:T(8,128)(2,1)} custom-call(bf16[128,3072]{1,0:T(8,128)(2,1)S(1)} %get-tuple-element.11.mixed_ref, bf16[128,1024]{1,0:T(8,128)(2,1)S(1)} %collective-permute-done.15.other_ref, bf16[1024,1024]{1,0:T(8,128)(2,1)S(1)} %get-tuple-element.12.key_w_ref, bf16[1024,1024]{1,0:T(8,128)(2,1)S(1)} %get-tuple-element.13.value_w_ref, ...), custom_call_target="tpu_custom_call" | custom-call | tf_op jit(solution)/shard_map/pallas_call | solution.py:489
Async XLA Ops:
  11.5 11.1 %collective-permute-start = (bf16[544,128]{1,0:T(8,128)(2,1)}, bf16[544,128]{1,0:T(8,128)(2,1)S(1)}, u32[]{:S(2)}, u32[]{:S(2)}) collective-permute-start(bf16[544,128]{1,0:T(8,128)(2,1)} %shard_map.127.refs_0_), channel_id=1, source_target_pairs={{0,16},{2,18},{4,20},{6,22},{8,24},{10,26},{12,28},{14,30},{16,0},... | collective-permute-start | bytes 417800 | tf_op jit(solution)/shard_map/ppermute | solution.py:218
  15.6 8.6 %collective-permute-start.3 = (bf16[544,128]{1,0:T(8,128)(2,1)}, bf16[544,128]{1,0:T(8,128)(2,1)S(1)}, u32[]{:S(2)}, u32[]{:S(2)}) collective-permute-start(bf16[544,128]{1,0:T(8,128)(2,1)} %shard_map.127.refs_0_), channel_id=1, source_target_pairs={{0,8},{2,10},{4,12},{6,14},{8,0},{10,2},{12,4},{14,6},{16,24},{18,... | collective-permute-start | bytes 417800 | tf_op jit(solution)/shard_map/ppermute | solution.py:218
  17.2 7.4 %collective-permute-start.1 = (bf16[544,128]{1,0:T(8,128)(2,1)}, bf16[544,128]{1,0:T(8,128)(2,1)S(1)}, u32[]{:S(2)}, u32[]{:S(2)}) collective-permute-start(bf16[544,128]{1,0:T(8,128)(2,1)} %shard_map.127.refs_0_), channel_id=1, source_target_pairs={{0,4},{2,6},{4,0},{6,2},{8,12},{10,14},{12,8},{14,10},{16,20},{18,... | collective-permute-start | bytes 417800 | tf_op jit(solution)/shard_map/ppermute | solution.py:218
  18.7 6.1 %collective-permute-start.7 = (bf16[544,128]{1,0:T(8,128)(2,1)}, bf16[544,128]{1,0:T(8,128)(2,1)S(1)}, u32[]{:S(2)}, u32[]{:S(2)}) collective-permute-start(bf16[544,128]{1,0:T(8,128)(2,1)} %shard_map.127.refs_0_), channel_id=1, source_target_pairs={{0,2},{2,0},{4,6},{6,4},{8,10},{10,8},{12,14},{14,12},{16,18},{18,... | collective-permute-start | bytes 417800 | tf_op jit(solution)/shard_map/ppermute | solution.py:218
  22.6 5.6 %collective-permute-start.2 = (bf16[544,128]{1,0:T(8,128)(2,1)S(1)}, bf16[544,128]{1,0:T(8,128)(2,1)S(1)}, u32[]{:S(2)}, u32[]{:S(2)}) collective-permute-start(bf16[544,128]{1,0:T(8,128)(2,1)S(1)} %collective-permute-done.refs_1_), channel_id=1, source_target_pairs={{0,4},{2,6},{4,0},{6,2},{8,12},{10,14},{12,8},{14,10},{16,20},{18,... | collective-permute-start | bytes 417800 | tf_op jit(solution)/shard_map/ppermute | solution.py:218
  24.2 5.7 %collective-permute-start.11 = (bf16[544,128]{1,0:T(8,128)(2,1)S(1)}, bf16[544,128]{1,0:T(8,128)(2,1)S(1)}, u32[]{:S(2)}, u32[]{:S(2)}) collective-permute-start(bf16[544,128]{1,0:T(8,128)(2,1)S(1)} %collective-permute-done.3.refs_4_), channel_id=1, source_target_pairs={{0,2},{2,0},{4,6},{6,4},{8,10},{10,8},{12,14},{14,12},{16,18},{18,... | collective-permute-start | bytes 417800 | tf_op jit(solution)/shard_map/ppermute | solution.py:218
  24.2 6.5 %collective-permute-start.5 = (bf16[544,128]{1,0:T(8,128)(2,1)S(1)}, bf16[544,128]{1,0:T(8,128)(2,1)S(1)}, u32[]{:S(2)}, u32[]{:S(2)}) collective-permute-start(bf16[544,128]{1,0:T(8,128)(2,1)S(1)} %collective-permute-done.3.refs_4_), channel_id=1, source_target_pairs={{0,4},{2,6},{4,0},{6,2},{8,12},{10,14},{12,8},{14,10},{16,20},{18,... | collective-permute-start | bytes 417800 | tf_op jit(solution)/shard_map/ppermute | solution.py:218
  24.6 6.0 %collective-permute-start.9 = (bf16[544,128]{1,0:T(8,128)(2,1)S(1)}, bf16[544,128]{1,0:T(8,128)(2,1)S(1)}, u32[]{:S(2)}, u32[]{:S(2)}) collective-permute-start(bf16[544,128]{1,0:T(8,128)(2,1)S(1)} %collective-permute-done.1.refs_2_), channel_id=1, source_target_pairs={{0,2},{2,0},{4,6},{6,4},{8,10},{10,8},{12,14},{14,12},{16,18},{18,... | collective-permute-start | bytes 417800 | tf_op jit(solution)/shard_map/ppermute | solution.py:218
  24.9 6.5 %collective-permute-start.4 = (bf16[544,128]{1,0:T(8,128)(2,1)S(1)}, bf16[544,128]{1,0:T(8,128)(2,1)S(1)}, u32[]{:S(2)}, u32[]{:S(2)}) collective-permute-start(bf16[544,128]{1,0:T(8,128)(2,1)S(1)} %collective-permute-done.refs_1_), channel_id=1, source_target_pairs={{0,8},{2,10},{4,12},{6,14},{8,0},{10,2},{12,4},{14,6},{16,24},{18,... | collective-permute-start | bytes 417800 | tf_op jit(solution)/shard_map/ppermute | solution.py:218
  28.2 5.5 %collective-permute-start.6 = (bf16[544,128]{1,0:T(8,128)(2,1)S(1)}, bf16[544,128]{1,0:T(8,128)(2,1)S(1)}, u32[]{:S(2)}, u32[]{:S(2)}) collective-permute-start(bf16[544,128]{1,0:T(8,128)(2,1)S(1)} %collective-permute-done.2.refs_3_), channel_id=1, source_target_pairs={{0,8},{2,10},{4,12},{6,14},{8,0},{10,2},{12,4},{14,6},{16,24},{18,... | collective-permute-start | bytes 417800 | tf_op jit(solution)/shard_map/ppermute | solution.py:218
  29.9 3.8 %collective-permute-start.8 = (bf16[544,128]{1,0:T(8,128)(2,1)S(1)}, bf16[544,128]{1,0:T(8,128)(2,1)S(1)}, u32[]{:S(2)}, u32[]{:S(2)}) collective-permute-start(bf16[544,128]{1,0:T(8,128)(2,1)S(1)} %collective-permute-done.refs_1_), channel_id=1, source_target_pairs={{0,2},{2,0},{4,6},{6,4},{8,10},{10,8},{12,14},{14,12},{16,18},{18,... | collective-permute-start | bytes 417800 | tf_op jit(solution)/shard_map/ppermute | solution.py:218
  30.6 3.1 %collective-permute-start.10 = (bf16[544,128]{1,0:T(8,128)(2,1)S(1)}, bf16[544,128]{1,0:T(8,128)(2,1)S(1)}, u32[]{:S(2)}, u32[]{:S(2)}) collective-permute-start(bf16[544,128]{1,0:T(8,128)(2,1)S(1)} %collective-permute-done.2.refs_3_), channel_id=1, source_target_pairs={{0,2},{2,0},{4,6},{6,4},{8,10},{10,8},{12,14},{14,12},{16,18},{18,... | collective-permute-start | bytes 417800 | tf_op jit(solution)/shard_map/ppermute | solution.py:218
  30.6 3.1 %collective-permute-start.13 = (bf16[544,128]{1,0:T(8,128)(2,1)S(1)}, bf16[544,128]{1,0:T(8,128)(2,1)S(1)}, u32[]{:S(2)}, u32[]{:S(2)}) collective-permute-start(bf16[544,128]{1,0:T(8,128)(2,1)S(1)} %collective-permute-done.5.refs_6_), channel_id=1, source_target_pairs={{0,2},{2,0},{4,6},{6,4},{8,10},{10,8},{12,14},{14,12},{16,18},{18,... | collective-permute-start | bytes 417800 | tf_op jit(solution)/shard_map/ppermute | solution.py:218
  31.4 2.3 %collective-permute-start.12 = (bf16[544,128]{1,0:T(8,128)(2,1)S(1)}, bf16[544,128]{1,0:T(8,128)(2,1)S(1)}, u32[]{:S(2)}, u32[]{:S(2)}) collective-permute-start(bf16[544,128]{1,0:T(8,128)(2,1)S(1)} %collective-permute-done.4.refs_5_), channel_id=1, source_target_pairs={{0,2},{2,0},{4,6},{6,4},{8,10},{10,8},{12,14},{14,12},{16,18},{18,... | collective-permute-start | bytes 417800 | tf_op jit(solution)/shard_map/ppermute | solution.py:218
  33.7 1.4 %collective-permute-start.14 = (bf16[544,128]{1,0:T(8,128)(2,1)S(1)}, bf16[544,128]{1,0:T(8,128)(2,1)S(1)}, u32[]{:S(2)}, u32[]{:S(2)}) collective-permute-start(bf16[544,128]{1,0:T(8,128)(2,1)S(1)} %collective-permute-done.6.refs_7_), channel_id=1, source_target_pairs={{0,2},{2,0},{4,6},{6,4},{8,10},{10,8},{12,14},{14,12},{16,18},{18,... | collective-permute-start | bytes 417800 | tf_op jit(solution)/shard_map/ppermute | solution.py:218
  35.1 0.9 %copy-start.1 = (bf16[544,128]{1,0:T(8,128)(2,1)S(1)}, bf16[544,128]{1,0:T(8,128)(2,1)}, u32[]{:S(2)}) copy-start(bf16[544,128]{1,0:T(8,128)(2,1)} %shard_map.127.refs_0_) | copy-start | bytes 417796
  37.7 8.4 %copy-start = (bf16[1024,1024]{1,0:T(8,128)(2,1)S(1)}, bf16[1024,1024]{1,0:T(8,128)(2,1)}, u32[]{:S(2)}) copy-start(bf16[1024,1024]{1,0:T(8,128)(2,1)} %out_w_hbm.1) | copy-start | bytes 6291460
  37.7 8.4 %copy-start.2 = (f32[4,16,64]{2,1,0:T(8,128)S(1)}, f32[4,16,64]{2,1,0:T(8,128)}, u32[]{:S(2)}) copy-start(f32[4,16,64]{2,1,0:T(8,128)} %bias_hbm.1) | copy-start | bytes 49156
  37.8 8.4 %collective-permute-start.15 = (bf16[128,1024]{1,0:T(8,128)(2,1)S(1)}, bf16[128,1024]{1,0:T(8,128)(2,1)S(1)}, u32[]{:S(2)}, u32[]{:S(2)}) collective-permute-start(bf16[128,1024]{1,0:T(8,128)(2,1)S(1)} %get-tuple-element.10.normed_ref), channel_id=1, source_target_pairs={{1,0},{0,1},{3,2},{2,3},{5,4},{4,5},{7,6},{6,7},{9,8},{8,9},{11,10... | collective-permute-start | bytes 786440 | tf_op jit(solution)/shard_map/ppermute | solution.py:526
